TPU v7x, 128 devices: a whole 4x4x4 slice. The times are simulated.
128 devices in a mesh: wide: 8 (over z, core), narrow: 16 (over y, x).
Axes of the slice: x: 4, y: 4, z: 4, core: 2. Of those that a mesh axis runs over, the one named last changes fastest.
Arguments:
- sources: bfloat16 [131072, 768], P(('wide', 'narrow')), as said below
- targets: bfloat16 [131072, 768], P(('wide', 'narrow')), as said below
- target_lists: int32 [1024, 4], P(('wide', 'narrow')), may hold values from 0 to 1023, as said below
- target_clusters: int32 [131072], P(('wide', 'narrow')), may hold values from 0 to 8191
- centroids_src: bfloat16 [8192, 768], P(('wide', 'narrow')), may hold values from -6 to 6
- centroids_tgt: bfloat16 [8192, 768], P('narrow', 'wide'), may hold values from -6 to 6
- sender_mean_measure: float32 [8192], P('wide'), may hold values from 0.05 to 20
- recipient_mean_measure: float32 [8192], P('narrow'), may hold values from 0.05 to 20
Outputs:
- src_bary: bfloat16 [131072, 768], P(('wide', 'narrow'))
- tgt_bary: bfloat16 [131072, 768], P(('wide', 'narrow'))
- src_potential: float32 [131072], P(('wide', 'narrow'))
- tgt_potential: float32 [131072], P(('wide', 'narrow'))
Inputs may be any that keep to these rules, and one draw needn't show every extreme that they name: `target_lists`: target block t holds targets t * 128 to (t + 1) * 128 - 1. Every entry names a block held by a device with the same wide index as the device of the source block. Among the 32 entries of one device, at most 3 name blocks held by any one device, and on every device some device is named by exactly 3. Every target block is named by at least one entry. `sources`: Real-valued features. `targets`: Real-valued features.
All inputs are finite; a program needn't handle non-finite values.
Results may differ from a plain program's by a relative error of at most 0.007.
Values may be sent and summed in bfloat16 or wider, within the bound.
No kernel may reach another device: no remote copies, remote signals or barrier semaphores. Data moves between devices by JAX's collectives and lax.ppermute only.
A program may use at most 128 MiB of HBM per device.

v0:
```python
import jax
import jax.numpy as jnp
from jax import lax
from jax.sharding import PartitionSpec as P

BLK = 128
LIST = 4
ITC = 6
STEPS = 3


heat_parameter = 0.02


def copy_for_each(value, axis):
    copies = jnp.broadcast_to(value, (lax.axis_size(axis), *value.shape))
    return lax.all_to_all(copies, axis, split_axis=0, concat_axis=0, tiled=True)


def all_in_one(value, axis):
    leaves = jax.tree.leaves(value)
    order = sorted(range(len(leaves)), key=lambda k: -leaves[k].size)
    width = (1, *leaves[order[0]].shape)[-1]
    lines = [
        jnp.pad(leaves[k].reshape(-1), (0, -leaves[k].size % width)).reshape(-1, width)
        for k in order
    ]
    both, at, found = (copy_for_each(jnp.concatenate(lines), axis), 0, {})
    for k, line in zip(order, lines):
        slab = both[:, at : at + len(line)].reshape(len(both), -1)
        found[k] = slab[:, : leaves[k].size].reshape(-1, *leaves[k].shape)
        at += len(line)
    numbers = iter(range(len(leaves)))
    return jax.tree.map(lambda _: found[next(numbers)], value)


def folded_in_pairs(pieces, combine):
    while len(jax.tree.leaves(pieces)[0]) > 1:
        pieces = jax.vmap(combine)(
            *(jax.tree.map(lambda part: part[side::2], pieces) for side in (0, 1))
        )
    return jax.tree.map(lambda part: part[0], pieces)


def joined_all(value, axis, combine):
    pieces = all_in_one(value, axis)
    return folded_in_pairs(pieces, combine)


def once_a_type(value, axis):
    leaves, found = (jax.tree.leaves(value), {})
    for leading, a in enumerate(leaves):
        if leading not in found:
            alike = [k for k, b in enumerate(leaves) if b.dtype == a.dtype]
            got = (
                all_in_one([leaves[k] for k in alike], axis)
                if len(alike) > 1
                else [copy_for_each(a, axis)]
            )
            for k, b in zip(alike, got):
                found[k] = b
    numbers = iter(range(len(leaves)))
    return jax.tree.map(lambda _: found[next(numbers)], value)


def combined_all(value, axis, combine):
    pieces = once_a_type(value, axis)
    return folded_in_pairs(pieces, combine)


def laid_out(blocks, dim):
    blocks = jnp.moveaxis(blocks, 0, dim)
    lengths = blocks.shape
    return blocks.reshape(*lengths[:dim], lengths[dim] * lengths[dim + 1], *lengths[dim + 2 :])


def gathered_copies(value, axis, dim):
    return laid_out(copy_for_each(value, axis), dim)


def side_by_side(arrays, axis, split_dim, concat_dim, along):
    widths = [a.shape[along] for a in arrays]
    both = jnp.concatenate(arrays, axis=along)
    out = lax.all_to_all(both, axis, split_axis=split_dim, concat_axis=concat_dim, tiled=True)
    return tuple(jnp.split(out, [sum(widths[:k]) for k in range(1, len(widths))], axis=along))


def contract_rows(left_rows, right_rows):
    return lax.dot_general(
        left_rows, right_rows, (((1,), (1,)), ((), ())), preferred_element_type=jnp.float32
    )


def square_norms(rows_in):
    return jnp.sum(jnp.square(rows_in.astype(jnp.float32)), axis=-1)


def combine_pair(first, second):
    best_rating = jnp.maximum(first[0], second[0])
    return (
        best_rating,
        first[1] * jnp.exp(first[0] - best_rating) + second[1] * jnp.exp(second[0] - best_rating),
    )


def lateral_lse_offset(rating_grid_form):
    best_rating = jnp.max(rating_grid_form, axis=1)
    ongoing_additions = jnp.sum(jnp.exp(rating_grid_form - best_rating[:, None]), axis=1)
    best_rating, ongoing_additions = joined_all(
        (best_rating, ongoing_additions), "narrow", combine_pair
    )
    return best_rating + jnp.log(ongoing_additions)


def vertical_lse_offset(rating_grid_form):
    best_rating = jnp.max(rating_grid_form, axis=0)
    ongoing_additions = jnp.sum(jnp.exp(rating_grid_form - best_rating[None, :]), axis=0)
    best_rating, ongoing_additions = combined_all(
        (best_rating, ongoing_additions), "wide", combine_pair
    )
    return best_rating + jnp.log(ongoing_additions)


def body(
    sources,
    targets,
    target_lists,
    target_clusters,
    centroids_src,
    centroids_tgt,
    sender_mean_measure,
    recipient_mean_measure,
):
    feature_count = sources.shape[1]
    narrow_count = lax.axis_size("narrow")
    col_panel = gathered_copies(centroids_tgt, "wide", 1)
    col_sq = square_norms(col_panel)
    fragment = gathered_copies(centroids_src, "narrow", 0)
    blurred_stratum = (
        square_norms(fragment)[:, None] + col_sq[None, :] - 2.0 * contract_rows(fragment, col_panel)
    ) / feature_count
    ln_sender_measure = heat_parameter * jnp.log(sender_mean_measure)
    ln_recipient_measure = heat_parameter * jnp.log(recipient_mean_measure)

    def coarse_turn(iteration, recipient_blurred_stratum):
        sender_blurred_stratum = ln_sender_measure - heat_parameter * lateral_lse_offset(
            (recipient_blurred_stratum[None, :] - blurred_stratum) / heat_parameter
        )
        return ln_recipient_measure - heat_parameter * vertical_lse_offset(
            (sender_blurred_stratum[:, None] - blurred_stratum) / heat_parameter
        )

    coarse_cols = lax.fori_loop(
        0, ITC, coarse_turn, jnp.zeros((blurred_stratum.shape[1],), jnp.float32)
    )
    coarse_all = gathered_copies(coarse_cols, "narrow", 0)
    src_blocks = sources.reshape(-1, BLK, feature_count)
    tgt_blocks = targets.reshape(-1, BLK, feature_count)
    src_count = src_blocks.shape[0]
    tgt_count = tgt_blocks.shape[0]
    capacity = max(
        (5 * src_count * LIST + 4 * narrow_count - 1) // (4 * narrow_count),
        (tgt_count + narrow_count - 1) // narrow_count,
    )
    slot_count = narrow_count * capacity
    wanted = target_lists.reshape(-1)
    entries = wanted.shape[0]
    entry_index = jnp.arange(entries, dtype=jnp.int32)
    owner_of = wanted // tgt_count % narrow_count
    local_block = wanted % tgt_count
    earlier = jnp.logical_and(
        owner_of[:, None] == owner_of[None, :], entry_index[None, :] < entry_index[:, None]
    )
    rank_of = jnp.sum(earlier.astype(jnp.int32), axis=1)
    slot_of = owner_of * capacity + rank_of
    requests = (
        jnp.full((slot_count,), -1, jnp.int32)
        .at[slot_of]
        .set(local_block)
        .reshape(narrow_count, capacity)
    )

    def into_slots(values):
        return jnp.zeros((slot_count,) + values.shape[1:], values.dtype).at[slot_of].set(values)

    asked_ids = lax.all_to_all(requests, "narrow", split_axis=0, concat_axis=0, tiled=True)
    found = jnp.take(tgt_blocks, jnp.clip(asked_ids, 0, tgt_count - 1), axis=0)
    received, asked_ids = (
        lax.all_to_all(
            jnp.where((asked_ids >= 0)[:, :, None, None], found, jnp.zeros((), jnp.bfloat16)),
            "narrow",
            split_axis=0,
            concat_axis=0,
            tiled=True,
        ),
        asked_ids,
    )
    rows_entry = jnp.take(
        received.reshape(slot_count, BLK, feature_count), slot_of, axis=0
    ).reshape(src_count, LIST, BLK, feature_count)
    src_sq = square_norms(src_blocks)
    rows_sq = square_norms(rows_entry)
    cross_term = jnp.einsum(
        "bid,blcd->blic", src_blocks, rows_entry, preferred_element_type=jnp.float32
    )
    pointwise_charge = (
        src_sq[:, None, :, None] + rows_sq[:, :, None, :] - 2.0 * cross_term
    ) / feature_count
    flat_asked = asked_ids.reshape(-1)
    slot_live = flat_asked >= 0
    clipped_asked = jnp.clip(flat_asked, 0, tgt_count - 1)
    slot_pick = flat_asked[None, :] == jnp.arange(tgt_count, dtype=jnp.int32)[:, None]
    recipient_kantorovich = jnp.take(coarse_all, target_clusters, axis=0).reshape(tgt_count, BLK)

    def send_potentials(values):
        outgoing = jnp.where(
            slot_live[:, None], jnp.take(values, clipped_asked, axis=0), 0.0
        ).reshape(narrow_count, capacity, BLK)
        back = lax.all_to_all(outgoing, "narrow", split_axis=0, concat_axis=0, tiled=True)
        return jnp.take(back.reshape(slot_count, BLK), slot_of, axis=0).reshape(
            src_count, LIST, BLK
        )

    sender_kantorovich = jnp.zeros((src_count, BLK), jnp.float32)
    for iteration in range(STEPS):
        named_kantorovich = send_potentials(recipient_kantorovich)
        rating_grid_form = (named_kantorovich[:, :, None, :] - pointwise_charge) / heat_parameter
        best_rating = jnp.max(rating_grid_form, axis=(1, 3))
        sender_kantorovich = -heat_parameter * (
            best_rating
            + jnp.log(
                jnp.sum(jnp.exp(rating_grid_form - best_rating[:, None, :, None]), axis=(1, 3))
            )
        )
        reverse_score_matrix = (
            sender_kantorovich[:, None, :, None] - pointwise_charge
        ) / heat_parameter
        part_top = jnp.max(reverse_score_matrix, axis=2)
        part_sum = jnp.sum(jnp.exp(reverse_score_matrix - part_top[:, :, None, :]), axis=2)
        top_slots = into_slots(part_top.reshape(entries, BLK)).reshape(narrow_count, capacity, BLK)
        sum_slots = into_slots(part_sum.reshape(entries, BLK)).reshape(narrow_count, capacity, BLK)
        top_back, sum_back = side_by_side((top_slots, sum_slots), "narrow", 0, 0, 1)
        flat_top = top_back.reshape(slot_count, BLK)
        flat_sum = sum_back.reshape(slot_count, BLK)
        largest_figure = jnp.max(
            jnp.where(slot_pick[:, :, None], flat_top[None, :, :], -jnp.inf), axis=1
        )
        ongoing_additions = jnp.sum(
            jnp.where(
                slot_pick[:, :, None],
                flat_sum[None, :, :] * jnp.exp(flat_top[None, :, :] - largest_figure[:, None, :]),
                0.0,
            ),
            axis=1,
        )
        recipient_kantorovich = -heat_parameter * (largest_figure + jnp.log(ongoing_additions))
    named_kantorovich = send_potentials(recipient_kantorovich)
    joint_measure_shares_entrywise = jnp.exp(
        (sender_kantorovich[:, None, :, None] + named_kantorovich[:, :, None, :] - pointwise_charge)
        / heat_parameter
    ).astype(jnp.bfloat16)
    src_num = jnp.einsum(
        "blic,blcd->bid",
        joint_measure_shares_entrywise,
        rows_entry,
        preferred_element_type=jnp.float32,
    )
    src_den = jnp.sum(joint_measure_shares_entrywise, axis=(1, 3), dtype=jnp.float32)
    src_bary = (src_num / src_den[:, :, None]).astype(jnp.bfloat16).reshape(-1, feature_count)
    entry_rows = jnp.einsum(
        "blic,bid->blcd",
        joint_measure_shares_entrywise,
        src_blocks,
        preferred_element_type=jnp.float32,
    ).astype(jnp.bfloat16)
    entry_mass = jnp.sum(joint_measure_shares_entrywise, axis=2, dtype=jnp.float32).astype(
        jnp.bfloat16
    )
    row_slots = into_slots(entry_rows.reshape(entries, BLK, feature_count)).reshape(
        narrow_count, capacity, BLK, feature_count
    )
    mass_slots = into_slots(entry_mass.reshape(entries, BLK)).reshape(narrow_count, capacity, BLK)
    numerator, denominator = (
        lax.all_to_all(row_slots, "narrow", split_axis=0, concat_axis=0, tiled=True),
        lax.all_to_all(mass_slots, "narrow", split_axis=0, concat_axis=0, tiled=True),
    )
    numerator = numerator.reshape(slot_count, BLK, feature_count)
    denominator = denominator.reshape(slot_count, BLK)
    picker = slot_pick.astype(jnp.bfloat16)
    tgt_num = jnp.dot(
        picker,
        numerator.reshape(slot_count, BLK * feature_count),
        preferred_element_type=jnp.float32,
    ).reshape(tgt_count, BLK, feature_count)
    tgt_den = jnp.dot(picker, denominator, preferred_element_type=jnp.float32)
    tgt_bary = (tgt_num / tgt_den[:, :, None]).astype(jnp.bfloat16).reshape(-1, feature_count)
    return (src_bary, tgt_bary, sender_kantorovich.reshape(-1), recipient_kantorovich.reshape(-1))


def solution(mesh):
    in_specs = (
        P(("wide", "narrow"), None),
        P(("wide", "narrow"), None),
        P(("wide", "narrow"), None),
        P(("wide", "narrow")),
        P(("wide", "narrow"), None),
        P("narrow", "wide"),
        P("wide"),
        P("narrow"),
    )
    out_specs = (
        P(("wide", "narrow"), None),
        P(("wide", "narrow"), None),
        P(("wide", "narrow")),
        P(("wide", "narrow")),
    )
    return jax.shard_map(body, mesh=mesh, in_specs=in_specs, out_specs=out_specs, check_vma=False)
```

profile of v0, /device:TPU:0, one launch (start us, length us, event | category | flops | bytes accessed | tf_op | source)
XLA Modules:
  0.0 683.1 jit_solution(2771796733561435213)
XLA Ops:
  2.7 14.5 %all_to_all.89 = s32[16,1,3]{2,1,0:T(1,128)S(1)} all-to-all(s32[16,1,3]{2,1,0:T(1,128)S(1)} %bitcast.162), channel_id=1, replica_groups=mesh['wide'=8,'narrow'=16] {'narrow'}, dimensions={0} | all-to-all | bytes 384 | tf_op jit(solution)/shard_map/all_to_all | solution.py:186
  24.4 13.1 %all-to-all-done.4 = bf16[8,512,96]{1,2,0:T(8,128)(2,1)S(1)} async-done(((bf16[8,512,96]{1,2,0:T(8,128)(2,1)}), bf16[8,512,96]{1,2,0:T(8,128)(2,1)S(1)}, u32[]{:S(2)}, u32[]{:S(2)}) %all-to-all-start.4) | async-done | bytes 786464 | tf_op jit(solution)/shard_map/all_to_all | solution.py:17
  45.6 21.5 %all-to-all-done.3 = bf16[16,64,768]{2,1,0:T(8,128)(2,1)S(1)} async-done(((bf16[16,64,768]{2,1,0:T(8,128)(2,1)}), bf16[16,64,768]{2,1,0:T(8,128)(2,1)S(1)}, u32[]{:S(2)}, u32[]{:S(2)}) %all-to-all-start.3) | async-done | bytes 1572896 | tf_op jit(solution)/shard_map/all_to_all | solution.py:17
  71.0 160.7 %while.11 = (s32[]{:T(128)}, f32[512]{0:T(512)S(1)}, f32[1024,512]{1,0:T(8,128)}, f32[1024]{0:T(1024)S(1)}, f32[512]{0:T(512)S(1)}, /*index=5*/s32[]{:T(128)}, s32[]{:T(128)}) while((s32[]{:T(128)}, f32[512]{0:T(512)S(1)}, f32[1024,512]{1,0:T(8,128)}, f32[1024]{0:T(1024)S(1)}, f32[512]{0:T(512)S(1)}, /*index=5*/s32[]{:T(128)}, ...), condition=%wide.region_9.10_spmd.clone, body=%wide.region_4.9_spmd.clone.sunk | while | flops 7458819 | bytes 27441324 | solution.py:153
  73.9 10.6 %all_to_all.95 = f32[16,2,1024]{2,1,0:T(2,128)S(1)} all-to-all(f32[16,2,1024]{2,1,0:T(2,128)S(1)} %broadcast_in_dim.358), channel_id=1, replica_groups=mesh['wide'=8,'narrow'=16] {'narrow'}, dimensions={0} | all-to-all | bytes 262144 | tf_op jit(solution)/shard_map/while/body/eval_jaxpr/all_to_all | solution.py:17
  91.7 5.4 all-to-all-done.1
  100.3 11.1 %all_to_all.95 = f32[16,2,1024]{2,1,0:T(2,128)S(1)} all-to-all(f32[16,2,1024]{2,1,0:T(2,128)S(1)} %broadcast_in_dim.358), channel_id=1, replica_groups=mesh['wide'=8,'narrow'=16] {'narrow'}, dimensions={0} | all-to-all | bytes 262144 | tf_op jit(solution)/shard_map/while/body/eval_jaxpr/all_to_all | solution.py:17
  118.6 5.4 all-to-all-done.1
  127.2 11.1 %all_to_all.95 = f32[16,2,1024]{2,1,0:T(2,128)S(1)} all-to-all(f32[16,2,1024]{2,1,0:T(2,128)S(1)} %broadcast_in_dim.358), channel_id=1, replica_groups=mesh['wide'=8,'narrow'=16] {'narrow'}, dimensions={0} | all-to-all | bytes 262144 | tf_op jit(solution)/shard_map/while/body/eval_jaxpr/all_to_all | solution.py:17
  145.4 5.4 all-to-all-done.1
  154.0 11.1 %all_to_all.95 = f32[16,2,1024]{2,1,0:T(2,128)S(1)} all-to-all(f32[16,2,1024]{2,1,0:T(2,128)S(1)} %broadcast_in_dim.358), channel_id=1, replica_groups=mesh['wide'=8,'narrow'=16] {'narrow'}, dimensions={0} | all-to-all | bytes 262144 | tf_op jit(solution)/shard_map/while/body/eval_jaxpr/all_to_all | solution.py:17
  180.9 11.1 %all_to_all.95 = f32[16,2,1024]{2,1,0:T(2,128)S(1)} all-to-all(f32[16,2,1024]{2,1,0:T(2,128)S(1)} %broadcast_in_dim.358), channel_id=1, replica_groups=mesh['wide'=8,'narrow'=16] {'narrow'}, dimensions={0} | all-to-all | bytes 262144 | tf_op jit(solution)/shard_map/while/body/eval_jaxpr/all_to_all | solution.py:17
  199.2 5.4 all-to-all-done.1
  207.8 11.1 %all_to_all.95 = f32[16,2,1024]{2,1,0:T(2,128)S(1)} all-to-all(f32[16,2,1024]{2,1,0:T(2,128)S(1)} %broadcast_in_dim.358), channel_id=1, replica_groups=mesh['wide'=8,'narrow'=16] {'narrow'}, dimensions={0} | all-to-all | bytes 262144 | tf_op jit(solution)/shard_map/while/body/eval_jaxpr/all_to_all | solution.py:17
  236.1 6.3 gather_fusion.1
  243.4 6.1 gather_fusion
  250.9 6.2 all-to-all-start.6
  257.1 8.5 %select_select_fusion = bf16[16,3,128,768]{3,2,1,0:T(8,128)(2,1)} fusion(bf16[16,3,128,768]{3,2,1,0:T(8,128)(2,1)} %bitcast.131, pred[16,3]{1,0:T(8,128)(4,1)S(1)} %copy.111, pred[16,3]{1,0:T(8,128)(4,1)S(1)} %bitcast.168), kind=kLoop, calls=%fused_computation.54 | loop fusion | flops 9437184 | bytes 18874464 | tf_op jit(solution)/shard_map/jit(_where)/select_n | solution.py:190
  265.6 7.4 %all-to-all-start.7 = ((bf16[16,3,128,768]{3,2,1,0:T(8,128)(2,1)}), bf16[16,3,128,768]{3,2,1,0:T(8,128)(2,1)}, u32[]{:S(2)}, u32[]{:S(2)}) async-start(bf16[16,3,128,768]{3,2,1,0:T(8,128)(2,1)} %select_select_fusion), calls=%async_computation.7 | async-start | bytes 18874368 | tf_op jit(solution)/shard_map/all_to_all | solution.py:189
  274.2 135.9 %all-to-all-done.7 = bf16[16,3,128,768]{3,2,1,0:T(8,128)(2,1)} async-done(((bf16[16,3,128,768]{3,2,1,0:T(8,128)(2,1)}), bf16[16,3,128,768]{3,2,1,0:T(8,128)(2,1)}, u32[]{:S(2)}, u32[]{:S(2)}) %all-to-all-start.7) | async-done | bytes 9437216 | tf_op jit(solution)/shard_map/all_to_all | solution.py:189
  410.1 7.2 %gather_fusion.2 = bf16[32,128,768]{2,1,0:T(8,128)(2,1)} fusion(bf16[48,128,768]{2,1,0:T(8,128)(2,1)} %bitcast.14, s32[1024]{0:T(1024)S(1)} %pad_clamp_fusion), kind=kCustom, calls=%fused_computation.10 | custom fusion | bytes 12583040 | tf_op jit(solution)/shard_map/jit(_take)/gather | solution.py:198
  430.3 5.8 all-to-all-start.8
  436.1 7.7 %all-to-all-done.8 = f32[16,6,128]{2,1,0:T(8,128)S(1)} async-done(((f32[16,6,128]{2,1,0:T(8,128)}), f32[16,6,128]{2,1,0:T(8,128)S(1)}, u32[]{:S(2)}, u32[]{:S(2)}) %all-to-all-start.8) | async-done | bytes 49184 | tf_op jit(solution)/shard_map/all_to_all | solution.py:84
  444.8 10.7 %all_to_all.90 = f32[16,3,128]{2,1,0:T(4,128)S(1)} all-to-all(f32[16,3,128]{2,1,0:T(4,128)S(1)} %reshape.526), channel_id=1, replica_groups=mesh['wide'=8,'narrow'=16] {'narrow'}, dimensions={0} | all-to-all | bytes 49152 | tf_op jit(solution)/shard_map/all_to_all | solution.py:219
  462.5 10.7 %all_to_all.91 = f32[16,6,128]{2,1,0:T(8,128)S(1)} all-to-all(f32[16,6,128]{2,1,0:T(8,128)S(1)} %pad_maximum_fusion.3), channel_id=1, replica_groups=mesh['wide'=8,'narrow'=16] {'narrow'}, dimensions={0} | all-to-all | bytes 98304 | tf_op jit(solution)/shard_map/all_to_all | solution.py:84
  474.3 10.7 %all_to_all.92 = f32[16,3,128]{2,1,0:T(4,128)S(1)} all-to-all(f32[16,3,128]{2,1,0:T(4,128)S(1)} %reshape.532), channel_id=1, replica_groups=mesh['wide'=8,'narrow'=16] {'narrow'}, dimensions={0} | all-to-all | bytes 49152 | tf_op jit(solution)/shard_map/all_to_all | solution.py:219
  493.2 10.7 %all_to_all.93 = f32[16,6,128]{2,1,0:T(8,128)S(1)} all-to-all(f32[16,6,128]{2,1,0:T(8,128)S(1)} %pad_maximum_fusion.4), channel_id=1, replica_groups=mesh['wide'=8,'narrow'=16] {'narrow'}, dimensions={0} | all-to-all | bytes 98304 | tf_op jit(solution)/shard_map/all_to_all | solution.py:84
  505.0 10.7 %all_to_all.94 = f32[16,3,128]{2,1,0:T(4,128)S(1)} all-to-all(f32[16,3,128]{2,1,0:T(4,128)S(1)} %reshape.538), channel_id=1, replica_groups=mesh['wide'=8,'narrow'=16] {'narrow'}, dimensions={0} | all-to-all | bytes 49152 | tf_op jit(solution)/shard_map/all_to_all | solution.py:219
  533.0 20.0 %scatter_fusion = bf16[48,128,768]{2,1,0:T(8,128)(2,1)} fusion(bf16[48,128,768]{2,1,0:T(8,128)(2,1)} %broadcast_in_dim.246, s32[32]{0:T(128)S(1)} %fusion.52, bf16[32,128,768]{2,1,0:T(8,128)(2,1)} %bitcast.134), kind=kCustom, calls=%fused_computation.18 | custom fusion | bytes 18874496 | tf_op jit(solution)/shard_map/scatter | solution.py:184
  553.0 7.2 %all-to-all-start.14 = ((bf16[16,3,128,768]{3,2,1,0:T(8,128)(2,1)}), bf16[16,3,128,768]{3,2,1,0:T(8,128)(2,1)}, u32[]{:S(2)}, u32[]{:S(2)}) async-start(bf16[16,3,128,768]{3,2,1,0:T(8,128)(2,1)} %bitcast.130), calls=%async_computation.14 | async-start | bytes 18874368 | tf_op jit(solution)/shard_map/all_to_all | solution.py:284
  565.8 105.3 %all-to-all-done.14 = bf16[16,3,128,768]{3,2,1,0:T(8,128)(2,1)} async-done(((bf16[16,3,128,768]{3,2,1,0:T(8,128)(2,1)}), bf16[16,3,128,768]{3,2,1,0:T(8,128)(2,1)}, u32[]{:S(2)}, u32[]{:S(2)}) %all-to-all-start.14) | async-done | bytes 9437216 | tf_op jit(solution)/shard_map/all_to_all | solution.py:284
  671.1 10.5 %divide_convert_fusion = bf16[8,128,768]{2,0,1:T(8,128)(2,1)S(1)} fusion(f32[8,128]{0,1:T(8,128)S(1)} %fusion.45, s32[48]{0:T(128)S(1)} %reshape.513, bf16[6,8,128,768]{3,2,1,0:T(8,128)(2,1)} %bitcast.59), kind=kOutput, calls=%fused_computation.61 | convolution fusion | flops 77070720 | bytes 11014336 | tf_op jit(solution)/shard_map/dot_general | solution.py:290
  (450 shorter events, 156.4 us)
Async XLA Ops:
  0.6 235.5 %copy-start = (bf16[1024,768]{1,0:T(8,128)(2,1)S(1)}, bf16[1024,768]{1,0:T(8,128)(2,1)}, u32[]{:S(2)}) copy-start(bf16[1024,768]{1,0:T(8,128)(2,1)} %param.15) | copy-start | bytes 4718596
  0.6 23.7 %copy-start.14 = (f32[1024]{0:T(1024)S(1)}, f32[1024]{0:T(1024)}, u32[]{:S(2)}) copy-start(f32[1024]{0:T(1024)} %param.20) | copy-start | bytes 12292
  0.7 23.8 %copy-start.13 = (s32[1024]{0:T(1024)S(1)}, s32[1024]{0:T(1024)}, u32[]{:S(2)}) copy-start(s32[1024]{0:T(1024)} %param.17) | copy-start | bytes 12292
  0.7 36.9 %copy-start.11 = (bf16[64,768]{1,0:T(8,128)(2,1)S(1)}, bf16[64,768]{1,0:T(8,128)(2,1)}, u32[]{:S(2)}) copy-start(bf16[64,768]{1,0:T(8,128)(2,1)} %param.18) | copy-start | bytes 294916
  19.1 18.4 %all-to-all-start.4 = ((bf16[8,512,96]{1,2,0:T(8,128)(2,1)}), bf16[8,512,96]{1,2,0:T(8,128)(2,1)S(1)}, u32[]{:S(2)}, u32[]{:S(2)}) async-start(bf16[8,512,96]{1,2,0:T(8,128)(2,1)} %broadcast_in_dim.226), calls=%async_computation.4 | async-start | bytes 1572864 | tf_op jit(solution)/shard_map/all_to_all | solution.py:17
  24.4 18.2 %copy-start.15 = (f32[512]{0:T(512)S(1)}, f32[512]{0:T(512)}, u32[]{:S(2)}) copy-start(f32[512]{0:T(512)} %param.21) | copy-start | bytes 6148
  38.9 28.2 %all-to-all-start.3 = ((bf16[16,64,768]{2,1,0:T(8,128)(2,1)}), bf16[16,64,768]{2,1,0:T(8,128)(2,1)S(1)}, u32[]{:S(2)}, u32[]{:S(2)}) async-start(bf16[16,64,768]{2,1,0:T(8,128)(2,1)} %broadcast_in_dim.225), calls=%async_computation.3 | async-start | bytes 3145728 | tf_op jit(solution)/shard_map/all_to_all | solution.py:17
  85.0 2.2 copy-start.3
  88.3 8.7 %all-to-all-start.1 = ((f32[8,2,512]{2,1,0:T(2,128)}), f32[8,2,512]{2,1,0:T(2,128)S(1)}, u32[]{:S(2)}, u32[]{:S(2)}) async-start(f32[8,2,512]{2,1,0:T(2,128)} %broadcast_in_dim.359), calls=%async_computation.1 | async-start | bytes 65536 | tf_op jit(solution)/shard_map/while/body/eval_jaxpr/all_to_all | solution.py:17
  97.4 2.2 copy-start.2
  111.9 2.2 copy-start.3
  115.2 8.7 %all-to-all-start.1 = ((f32[8,2,512]{2,1,0:T(2,128)}), f32[8,2,512]{2,1,0:T(2,128)S(1)}, u32[]{:S(2)}, u32[]{:S(2)}) async-start(f32[8,2,512]{2,1,0:T(2,128)} %broadcast_in_dim.359), calls=%async_computation.1 | async-start | bytes 65536 | tf_op jit(solution)/shard_map/while/body/eval_jaxpr/all_to_all | solution.py:17
  138.7 2.2 copy-start.3
  142.1 8.7 %all-to-all-start.1 = ((f32[8,2,512]{2,1,0:T(2,128)}), f32[8,2,512]{2,1,0:T(2,128)S(1)}, u32[]{:S(2)}, u32[]{:S(2)}) async-start(f32[8,2,512]{2,1,0:T(2,128)} %broadcast_in_dim.359), calls=%async_computation.1 | async-start | bytes 65536 | tf_op jit(solution)/shard_map/while/body/eval_jaxpr/all_to_all | solution.py:17
  165.6 2.2 copy-start.3
  169.0 8.7 %all-to-all-start.1 = ((f32[8,2,512]{2,1,0:T(2,128)}), f32[8,2,512]{2,1,0:T(2,128)S(1)}, u32[]{:S(2)}, u32[]{:S(2)}) async-start(f32[8,2,512]{2,1,0:T(2,128)} %broadcast_in_dim.359), calls=%async_computation.1 | async-start | bytes 65536 | tf_op jit(solution)/shard_map/while/body/eval_jaxpr/all_to_all | solution.py:17
  192.5 2.2 copy-start.3
  195.8 8.7 %all-to-all-start.1 = ((f32[8,2,512]{2,1,0:T(2,128)}), f32[8,2,512]{2,1,0:T(2,128)S(1)}, u32[]{:S(2)}, u32[]{:S(2)}) async-start(f32[8,2,512]{2,1,0:T(2,128)} %broadcast_in_dim.359), calls=%async_computation.1 | async-start | bytes 65536 | tf_op jit(solution)/shard_map/while/body/eval_jaxpr/all_to_all | solution.py:17
  219.3 2.2 copy-start.3
  222.7 8.7 %all-to-all-start.1 = ((f32[8,2,512]{2,1,0:T(2,128)}), f32[8,2,512]{2,1,0:T(2,128)S(1)}, u32[]{:S(2)}, u32[]{:S(2)}) async-start(f32[8,2,512]{2,1,0:T(2,128)} %broadcast_in_dim.359), calls=%async_computation.1 | async-start | bytes 65536 | tf_op jit(solution)/shard_map/while/body/eval_jaxpr/all_to_all | solution.py:17
  232.4 11.0 %all-to-all-start.5 = ((f32[16,1,512]{2,1,0:T(1,128)}), f32[16,1,512]{2,1,0:T(1,128)S(1)}, u32[]{:S(2)}, u32[]{:S(2)}) async-start(f32[16,1,512]{2,1,0:T(1,128)} %broadcast_in_dim.227), calls=%async_computation.5 | async-start | bytes 65536 | tf_op jit(solution)/shard_map/all_to_all | solution.py:17
  250.9 14.7 %all-to-all-start.6 = ((f32[16,3,128]{2,1,0:T(4,128)}), f32[16,3,128]{2,1,0:T(4,128)S(1)}, u32[]{:S(2)}, u32[]{:S(2)}) async-start(f32[16,3,128]{2,1,0:T(4,128)} %reshape.517), calls=%async_computation.6 | async-start | bytes 65536 | tf_op jit(solution)/shard_map/all_to_all | solution.py:219
  265.6 7.5 %copy-start.9 = (bf16[1024,768]{1,0:T(8,128)(2,1)S(1)}, bf16[1024,768]{1,0:T(8,128)(2,1)}, u32[]{:S(2)}) copy-start(bf16[1024,768]{1,0:T(8,128)(2,1)} %param.14) | copy-start | bytes 4718596
  265.6 144.5 %all-to-all-start.7 = ((bf16[16,3,128,768]{3,2,1,0:T(8,128)(2,1)}), bf16[16,3,128,768]{3,2,1,0:T(8,128)(2,1)}, u32[]{:S(2)}, u32[]{:S(2)}) async-start(bf16[16,3,128,768]{3,2,1,0:T(8,128)(2,1)} %select_select_fusion), calls=%async_computation.7 | async-start | bytes 18874368 | tf_op jit(solution)/shard_map/all_to_all | solution.py:189
  417.3 4.7 copy-start.7
  430.3 13.5 %all-to-all-start.8 = ((f32[16,6,128]{2,1,0:T(8,128)}), f32[16,6,128]{2,1,0:T(8,128)S(1)}, u32[]{:S(2)}, u32[]{:S(2)}) async-start(f32[16,6,128]{2,1,0:T(8,128)} %pad_maximum_fusion.2), calls=%async_computation.8 | async-start | bytes 131072 | tf_op jit(solution)/shard_map/all_to_all | solution.py:84
  485.7 4.1 copy-start.6
  489.8 26.6 %copy-start.12 = (f32[8,128]{1,0:T(8,128)}, f32[8,128]{1,0:T(8,128)S(1)}, u32[]{:S(2)}) copy-start(f32[8,128]{1,0:T(8,128)S(1)} %add_multiply_fusion.3) | copy-start | bytes 12292
  504.3 23.9 %copy-start.8 = (f32[8,128]{1,0:T(8,128)}, f32[8,128]{1,0:T(8,128)S(1)}, u32[]{:S(2)}) copy-start(f32[8,128]{1,0:T(8,128)S(1)} %add_multiply_fusion.2) | copy-start | bytes 12292
  520.2 32.8 %all-to-all-start.15 = ((bf16[16,3,128]{2,1,0:T(4,128)(2,1)}), bf16[16,3,128]{2,1,0:T(4,128)(2,1)S(1)}, u32[]{:S(2)}, u32[]{:S(2)}) async-start(bf16[16,3,128]{2,1,0:T(4,128)(2,1)} %reshape.544), calls=%async_computation.15 | async-start | bytes 32768 | tf_op jit(solution)/shard_map/all_to_all | solution.py:285
  553.0 118.1 %all-to-all-start.14 = ((bf16[16,3,128,768]{3,2,1,0:T(8,128)(2,1)}), bf16[16,3,128,768]{3,2,1,0:T(8,128)(2,1)}, u32[]{:S(2)}, u32[]{:S(2)}) async-start(bf16[16,3,128,768]{3,2,1,0:T(8,128)(2,1)} %bitcast.130), calls=%async_computation.14 | async-start | bytes 18874368 | tf_op jit(solution)/shard_map/all_to_all | solution.py:284
  671.1 12.0 %copy-start.1 = (bf16[1024,768]{1,0:T(8,128)(2,1)S(1)}, bf16[1024,768]{1,0:T(8,128)(2,1)}, u32[]{:S(2)}) copy-start(bf16[1024,768]{1,0:T(8,128)(2,1)} %param.15) | copy-start | bytes 4718596
  (8 other events, 16.1 us)
where the time goes:
time: 685 us; the launch traced here: 683 us
  waiting for transfers between devices  317 us (46%)
  blocking collectives  134 us (20%)
  local copies, waits for them, and re-layouts  73.5 us (11%)
  other arithmetic  66.4 us (10%)
  starting transfers between devices  62.7 us (9%)
  matrix products  27.3 us (4%)
    all_to_all x1, waiting for transfers between devices, body(): lax.all_to_all(jnp.where((asked_ids >= 0)[:, :, None, None], found, jnp.z...  136 us
    all_to_all x1, waiting for transfers between devices, body(): lax.all_to_all(row_slots, 'narrow', split_axis=0, concat_axis=0, tiled=True)  105 us
    all_to_all x9, waiting for transfers between devices, copy_for_each(): return lax.all_to_all(copies, axis, split_axis=0, concat_axis=0, tiled=True)  67.7 us
    all_to_all x6, blocking collectives, copy_for_each(): return lax.all_to_all(copies, axis, split_axis=0, concat_axis=0, tiled=True)  65.9 us
    all_to_all x9, starting transfers between devices, copy_for_each(): return lax.all_to_all(copies, axis, split_axis=0, concat_axis=0, tiled=True)  32.6 us
    all_to_all x3, blocking collectives, send_potentials(): lax.all_to_all(outgoing, 'narrow', split_axis=0, concat_axis=0, tiled=True)  32.2 us
    scatter x8, local copies, waits for them, and re-layouts, into_slots(): jnp.zeros((slot_count,) + values.shape[1:], values.dtype).at[slot_of]  24.7 us
    all_to_all x2, blocking collectives, side_by_side(): lax.all_to_all(both, axis, split_axis=split_dim, concat_axis=concat_dim,...  21.5 us
  transfers between devices with their start and end apart: 14, of which 12 were waited for; matrix products, arithmetic and copies ran while one was open for 8% of the time, Pallas kernels for 0%

commit v1 on v0

v1 whole, which is shorter than its diff:
```python
import functools

import jax
import jax.numpy as jnp
from jax import lax
from jax.experimental import pallas as pl
from jax.experimental.pallas import tpu as pltpu
from jax.sharding import Mesh
from jax.sharding import PartitionSpec as P

BLK = 128
LIST = 4
ITC = 6
STEPS = 3
CAP = 3
HEAT = 0.02
SIDE = 4
OWN = 8
GROUP = SIDE * OWN
UNROLL = 4
SLOTS = SIDE * SIDE * CAP + UNROLL
HALF = OWN // 2
HALF_ROWS = HALF * BLK + 16
FAR = (4, 5)
NEAR = (2, 7, 3, 6, 0, 1)
NEG = -1e30
AT_SRC, AT_TGT, AT_START, AT_COUNT, AT_LIST, AT_LIVE, TABLE = 0, 64, 128, 168, 200, 712, 768
LINES = 3 * OWN + 1

F32 = jnp.float32
BF16 = jnp.bfloat16


def spec(n):
    return [pl.BlockSpec(memory_space=pltpu.VMEM)] * n


def smem(n):
    return [pl.BlockSpec(memory_space=pltpu.SMEM)] * n


def columns_of(rows):
    count = rows.shape[0]
    if count < BLK:
        rows = jnp.concatenate([rows, jnp.zeros((BLK - count, BLK), F32)], axis=0)
    return rows.T


def spread(col_ref, columns, count):
    for k in range(count):
        col_ref[k] = jnp.broadcast_to(columns[:, k : k + 1], (BLK, BLK))


def joined(parts_ref):
    count = parts_ref.shape[0]
    top = parts_ref[0]
    for k in range(1, count):
        top = jnp.maximum(top, parts_ref[k])
    total = jnp.exp(parts_ref[0] - top)
    for k in range(1, count):
        total = total + jnp.exp(parts_ref[k] - top)
    return top + jnp.log(total)


def tree(parts, op):
    while len(parts) > 1:
        parts = [op(a, b) for a, b in zip(parts[::2], parts[1::2])] + (
            [parts[-1]] if len(parts) % 2 else []
        )
    return parts[0]


def coarse_cost_kernel(scale, place_ref, x_ref, *refs):
    pieces, (by_col_ref, by_row_ref, y_ref, ysq_ref) = refs[:SIDE], refs[SIDE:]
    z, core = place_ref[2], place_ref[3]
    depth, cols = pieces[0].shape[1], y_ref.shape[1] // BLK
    for away in range(SIDE):
        home = lax.rem(z + SIDE - away, SIDE) * 2
        for twin in range(2):
            at = (home + lax.rem(core + twin, 2)) * depth
            y_ref[pl.ds(pl.multiple_of(at, depth), depth), :] = pieces[away][twin]
    for k in range(cols):
        wide_y = y_ref[:, k * BLK : (k + 1) * BLK].astype(F32)
        ysq_ref[k : k + 1, :] = jnp.sum(wide_y * wide_y, axis=0, keepdims=True)
    tall = 2 * BLK

    def one(j, carry):
        x = x_ref[pl.ds(pl.multiple_of(j * tall, tall), tall), :]
        wide_x = x.astype(F32)
        x_sq = jnp.sum(wide_x * wide_x, axis=1, keepdims=True)
        for k in range(cols):
            y = y_ref[:, k * BLK : (k + 1) * BLK]
            cross = jnp.dot(x, y, preferred_element_type=F32)
            cost = (x_sq + ysq_ref[k : k + 1, :] - 2.0 * cross) * scale
            by_col_ref[k, pl.ds(pl.multiple_of(j * tall, tall), tall), :] = cost
            for h in range(2):
                by_row_ref[2 * j + h, k * BLK : (k + 1) * BLK, :] = cost[
                    h * BLK : (h + 1) * BLK, :
                ].T
        return carry

    lax.fori_loop(0, x_ref.shape[0] // tall, one, 0)


def coarse_costs(place, x, pieces, scale):
    rows, cols = x.shape[0] // BLK, pieces[0].shape[2] // BLK
    return pl.pallas_call(
        functools.partial(coarse_cost_kernel, scale),
        out_shape=(
            jax.ShapeDtypeStruct((cols, rows * BLK, BLK), F32),
            jax.ShapeDtypeStruct((rows, cols * BLK, BLK), F32),
        ),
        in_specs=smem(1) + spec(1 + SIDE),
        out_specs=tuple(spec(2)),
        scratch_shapes=[
            pltpu.VMEM((x.shape[1], cols * BLK), BF16),
            pltpu.VMEM((8, BLK), F32),
        ],
        compiler_params=pltpu.CompilerParams(vmem_limit_bytes=20 << 20),
        name="coarse_costs",
    )(place, x, *pieces)


def coarse_half_kernel(first, recv_ref, mass_ref, cost_ref, out_ref, col_ref, res_ref):
    given = mass_ref.shape[0]
    chunks = cost_ref.shape[0]
    if first:
        potential = jnp.zeros((given, BLK), F32)
    else:
        potential = jnp.log(mass_ref[...]) - joined(recv_ref)
    spread(col_ref, columns_of(potential), given)

    def chunk(c, carry):
        def piece(k):
            cost = cost_ref[c, k * BLK : (k + 1) * BLK, :]
            return (col_ref[k] - cost).reshape(BLK // 8, 8, BLK)

        top = tree([jnp.max(piece(k), axis=0) for k in range(given)], jnp.maximum)
        total = tree(
            [jnp.sum(jnp.exp(piece(k) - top[None]), axis=0) for k in range(given)], jnp.add
        )
        best = jnp.max(top, axis=0, keepdims=True)
        total = jnp.sum(total * jnp.exp(top - best), axis=0, keepdims=True)
        res_ref[pl.ds(c, 1), :] = best + jnp.log(total)
        return carry

    lax.fori_loop(0, chunks, chunk, 0)
    result = res_ref[0:chunks, :]
    for k in range(out_ref.shape[0]):
        out_ref[k] = result


def coarse_half(first, recv, mass, cost, copies):
    given, chunks = mass.shape[0], cost.shape[0]
    return pl.pallas_call(
        functools.partial(coarse_half_kernel, first),
        out_shape=jax.ShapeDtypeStruct((copies, chunks, BLK), F32),
        in_specs=spec(3),
        out_specs=spec(1)[0],
        scratch_shapes=[pltpu.VMEM((given, BLK, BLK), F32), pltpu.VMEM((8, BLK), F32)],
        compiler_params=pltpu.CompilerParams(vmem_limit_bytes=12 << 20),
        name="coarse_half",
    )(recv, mass, cost)


def coarse_end_kernel(recv_ref, mass_ref, out_ref):
    potential = jnp.log(mass_ref[...]) - joined(recv_ref)
    for k in range(out_ref.shape[0]):
        out_ref[k] = potential


def coarse_end(recv, mass, copies):
    return pl.pallas_call(
        coarse_end_kernel,
        out_shape=jax.ShapeDtypeStruct((copies, *mass.shape), F32),
        in_specs=spec(2),
        out_specs=spec(1)[0],
        name="coarse_end",
    )(recv, mass)


def plan_kernel(lists_ref, place_ref, table_ref):
    y = place_ref[0]

    def clear(k, carry):
        for j in range(8):
            table_ref[k * 8 + j] = 0
        return carry

    lax.fori_loop(0, TABLE // 8, clear, 0)

    def scan(q, live):
        block = lists_ref[q]
        device = lax.rem(lax.div(block, OWN), SIDE * SIDE)
        here = (lax.div(device, SIDE) == y).astype(jnp.int32)
        s = lax.div(q, LIST)
        t = lax.rem(device, SIDE) * OWN + lax.rem(block, OWN)
        table_ref[AT_SRC + live] = s
        table_ref[AT_TGT + live] = t
        seen = table_ref[AT_COUNT + t]
        table_ref[AT_LIST + t * 16 + seen] = live
        table_ref[AT_COUNT + t] = seen + here
        live = live + here
        table_ref[AT_START + s + 1] = live
        return live

    live = lax.fori_loop(0, SIDE * OWN * LIST, scan, 0)
    for k in range(UNROLL + 1):
        table_ref[AT_SRC + live + k] = GROUP
        table_ref[AT_TGT + live + k] = GROUP
    table_ref[AT_LIVE] = live


def entry_table(lists, place):
    return pl.pallas_call(
        plan_kernel,
        out_shape=jax.ShapeDtypeStruct((TABLE,), jnp.int32),
        in_specs=smem(2),
        out_specs=smem(1)[0],
        name="entry_table",
    )(lists, place)


def fine_cost_kernel(scale, table_ref, x_ref, y_ref, xsq_ref, ysq_ref, a_ref, at_ref, col_ref):
    spread(col_ref, columns_of(xsq_ref[...]), GROUP)

    def some(r, carry):
        for k in range(UNROLL):
            e = r * UNROLL + k
            s = jnp.minimum(table_ref[AT_SRC + e], GROUP - 1)
            t = jnp.minimum(table_ref[AT_TGT + e], GROUP - 1)
            cross = lax.dot_general(
                x_ref[s], y_ref[t], (((1,), (1,)), ((), ())), preferred_element_type=F32
            )
            cost = (col_ref[s] + ysq_ref[pl.ds(t, 1), :] - 2.0 * cross) * scale
            a_ref[e] = cost
            at_ref[e] = cost.T
        return carry

    lax.fori_loop(0, lax.div(table_ref[AT_LIVE] + (UNROLL - 1), UNROLL), some, 0)


def fine_costs(table, x, y, xsq, ysq, scale):
    shape = jax.ShapeDtypeStruct((SLOTS, BLK, BLK), F32)
    return pl.pallas_call(
        functools.partial(fine_cost_kernel, scale),
        out_shape=(shape, shape),
        in_specs=smem(1) + spec(4),
        out_specs=tuple(spec(2)),
        scratch_shapes=[pltpu.VMEM((GROUP, BLK, BLK), F32)],
        name="fine_costs",
    )(table, x, y, xsq, ysq)


def looked_up(coarse_ref, ids_ref, pot_ref):
    rows = coarse_ref.shape[0]
    by_lane = columns_of(coarse_ref[...])[:, :rows]
    high = by_lane.astype(BF16)
    rest = by_lane - high.astype(F32)
    middle = rest.astype(BF16)
    low = (rest - middle.astype(F32)).astype(BF16)
    parts = jnp.concatenate([high, middle, low, jnp.zeros_like(low)], axis=1)
    depth = 4 * rows
    row_at = lax.rem(lax.broadcasted_iota(jnp.int32, (depth, BLK), 0), rows)
    lane_at = lax.broadcasted_iota(jnp.int32, (BLK, BLK), 0)

    def some(r, carry):
        for k in range(UNROLL):
            ids = ids_ref[pl.ds(r * UNROLL + k, 1), :]
            pick = jnp.where(row_at == (ids >> 7), 1.0, 0.0).astype(BF16)
            found = jnp.dot(parts, pick, preferred_element_type=F32)
            pot_ref[pl.ds(r * UNROLL + k, 1), :] = jnp.sum(
                jnp.where(lane_at == (ids & (BLK - 1)), found, 0.0), axis=0, keepdims=True
            )
        return carry

    lax.fori_loop(0, GROUP // UNROLL, some, 0)


def fine_half_kernel(first, given_at, into_at, *refs):
    if first:
        table_ref, coarse_ref, ids_ref, mat_ref, out_ref, col_ref, top_ref, sum_ref = refs
        looked_up(coarse_ref, ids_ref, top_ref)
        potential = top_ref[0:GROUP, :]
    else:
        table_ref, recv_ref, mat_ref, out_ref, col_ref, top_ref, sum_ref = refs
        potential = -joined(recv_ref)
    spread(col_ref, columns_of(potential), GROUP)
    top_ref[...] = jnp.full(top_ref.shape, NEG, F32)
    sum_ref[...] = jnp.zeros(sum_ref.shape, F32)

    def some(r, carry):
        found = []
        for k in range(UNROLL):
            e = r * UNROLL + k
            given = jnp.minimum(table_ref[given_at + e], GROUP - 1)
            rating = (col_ref[given] - mat_ref[e]).reshape(BLK // 8, 8, BLK)
            top = jnp.max(rating, axis=0)
            total = jnp.sum(jnp.exp(rating - top[None]), axis=0)
            best = jnp.max(top, axis=0, keepdims=True)
            found.append((best, jnp.sum(total * jnp.exp(top - best), axis=0, keepdims=True)))
        for k in range(UNROLL):
            into = table_ref[into_at + r * UNROLL + k]
            row = pl.ds(into, 1)
            best, total = found[k]
            before = top_ref[row, :]
            now = jnp.maximum(before, best)
            sum_ref[row, :] = sum_ref[row, :] * jnp.exp(before - now) + total * jnp.exp(best - now)
            top_ref[row, :] = now
        return carry

    lax.fori_loop(0, lax.div(table_ref[AT_LIVE] + (UNROLL - 1), UNROLL), some, 0)
    result = top_ref[0:GROUP, :] + jnp.log(sum_ref[0:GROUP, :])
    for k in range(SIDE):
        out_ref[k] = result


def fine_half(first, given_at, into_at, table, given, mat):
    return pl.pallas_call(
        functools.partial(fine_half_kernel, first, given_at, into_at),
        out_shape=jax.ShapeDtypeStruct((SIDE, GROUP, BLK), F32),
        in_specs=smem(1) + spec(len(given) + 1),
        out_specs=spec(1)[0],
        scratch_shapes=[
            pltpu.VMEM((GROUP, BLK, BLK), F32),
            pltpu.VMEM((GROUP + 8, BLK), F32),
            pltpu.VMEM((GROUP + 8, BLK), F32),
        ],
        compiler_params=pltpu.CompilerParams(vmem_limit_bytes=16 << 20),
        name="fine_half",
    )(table, *given, mat)


def own_kernel(place_ref, srecv_ref, trecv_ref, s_ref, t_ref, sown_ref, town_ref):
    s_ref[...] = -joined(srecv_ref)
    t_ref[...] = -joined(trecv_ref)
    own_s = pl.ds(pl.multiple_of(place_ref[0] * OWN, OWN), OWN)
    own_t = pl.ds(pl.multiple_of(place_ref[1] * OWN, OWN), OWN)
    sown_ref[...] = HEAT * s_ref[own_s, :]
    town_ref[...] = HEAT * t_ref[own_t, :]


def final_potentials(place, srecv, trecv):
    some = jax.ShapeDtypeStruct((GROUP, BLK), F32)
    own = jax.ShapeDtypeStruct((OWN, BLK), F32)
    return pl.pallas_call(
        own_kernel,
        out_shape=(some, some, own, own),
        in_specs=smem(1) + spec(2),
        out_specs=tuple(spec(4)),
        compiler_params=pltpu.CompilerParams(vmem_limit_bytes=4 << 20),
        name="final_potentials",
    )(place, srecv, trecv)


def masses_put(buf, at, mass, width):
    high = mass.astype(BF16).astype(F32)
    both = jnp.concatenate([high, mass - high, jnp.zeros((8, width - 2 * BLK), F32)], axis=1)
    buf[at, HALF * BLK :, :] = jnp.concatenate([both, jnp.zeros_like(both)], axis=0).astype(BF16)


def masses_of(tail):
    return tail[:, 0:BLK].astype(F32) + tail[:, BLK : 2 * BLK].astype(F32)


def sums_kernel(by_src, table_ref, place_ref, picks_ref, mine_ref, other_ref, mat_ref, rows_ref, out_ref, acc_ref, mass_ref):
    q = pl.program_id(0)
    away, half = lax.div(picks_ref[q], 2), lax.rem(picks_ref[q], 2)
    base = lax.rem(place_ref[0 if by_src else 1] + away, SIDE) * OWN + half * HALF
    ones = jnp.ones((8, BLK), BF16)
    partner = AT_TGT if by_src else AT_SRC

    def term(block, k, column, live):
        if by_src:
            e = table_ref[AT_START + block] + k
        else:
            e = table_ref[AT_LIST + block * 16 + k]
        peer = jnp.minimum(table_ref[partner + e], GROUP - 1)
        plan = jnp.exp(column + other_ref[pl.ds(peer, 1), :] - mat_ref[e])
        if live is not None:
            plan = jnp.where(live, plan, 0.0)
        plan = plan.astype(BF16)
        total = jnp.dot(plan, rows_ref[peer], preferred_element_type=F32)
        mass = lax.dot_general(ones, plan, (((1,), (1,)), ((), ())), preferred_element_type=F32)
        return total, mass[0:1, :]

    columns, counts = [], []
    for b in range(HALF):
        block = base + b
        if by_src:
            count = table_ref[AT_START + block + 1] - table_ref[AT_START + block]
        else:
            count = table_ref[AT_COUNT + block]
        column = jnp.broadcast_to(mine_ref[pl.ds(block, 1), :], (BLK, BLK)).T
        total, mass = term(block, 0, column, count > 0)
        acc_ref[b] = total
        mass_ref[b : b + 1, :] = mass
        counts.append(count)
    for b in range(HALF):

        def more(k, carry, b=b):
            column = jnp.broadcast_to(mine_ref[pl.ds(base + b, 1), :], (BLK, BLK)).T
            total, mass = term(base + b, k, column, None)
            acc_ref[b] += total
            mass_ref[b : b + 1, :] += mass
            return carry

        lax.fori_loop(1, counts[b], more, 0)
    for b in range(HALF):
        out_ref[0, b * BLK : (b + 1) * BLK, :] = acc_ref[b].astype(BF16)
    masses_put(out_ref, 0, mass_ref[...], out_ref.shape[2])


def weighted_sums(by_src, picks, table, place, mine, other, mat, rows):
    width = rows.shape[2]
    return pl.pallas_call(
        functools.partial(sums_kernel, by_src),
        out_shape=jax.ShapeDtypeStruct((len(picks), HALF_ROWS, width), BF16),
        grid=(len(picks),),
        in_specs=smem(3) + spec(4),
        out_specs=pl.BlockSpec((1, HALF_ROWS, width), lambda q: (q, 0, 0)),
        scratch_shapes=[pltpu.VMEM((HALF, BLK, width), F32), pltpu.VMEM((8, BLK), F32)],
        compiler_params=pltpu.CompilerParams(vmem_limit_bytes=24 << 20),
        name="weighted_sums",
    )(table, place, jnp.array(picks, jnp.int32), mine, other, mat, rows)


def add_kernel(a_ref, b_ref, out_ref):
    for b in range(HALF):
        rows = slice(b * BLK, (b + 1) * BLK)
        out_ref[0, rows, :] = (a_ref[0, rows, :].astype(F32) + b_ref[0, rows, :].astype(F32)).astype(BF16)
    tail = slice(HALF * BLK, HALF_ROWS)
    mass = masses_of(a_ref[0, tail, :]) + masses_of(b_ref[0, tail, :])
    masses_put(out_ref, 0, mass[0:8, :], out_ref.shape[2])


def added(a, b):
    return pl.pallas_call(
        add_kernel,
        out_shape=jax.ShapeDtypeStruct(a.shape, BF16),
        in_specs=spec(2),
        out_specs=spec(1)[0],
        compiler_params=pltpu.CompilerParams(vmem_limit_bytes=8 << 20),
        name="added",
    )(a, b)


def mean_kernel(*refs):
    ins, out_ref = refs[:-1], refs[-1]
    step = pl.program_id(0)

    def give(rows, tails, b):
        mass = masses_of(tails[0][0])
        total = rows[0][0].astype(F32)
        for row, tail in zip(rows[1:], tails[1:]):
            mass = mass + masses_of(tail[0])
            total = total + row[0].astype(F32)
        pick = lax.broadcasted_iota(jnp.int32, mass.shape, 0) == b
        line = jnp.sum(jnp.where(pick, mass, 0.0), axis=0, keepdims=True)
        share = jnp.broadcast_to(1.0 / line, (BLK, BLK)).T
        out_ref[...] = (total * share[:, 0:1]).astype(BF16)

    @pl.when(step < HALF)
    def _():
        give(ins[0:3], ins[6:9], step)

    @pl.when(step >= HALF)
    def _():
        give(ins[3:6], ins[9:12], step - HALF)


def mean_of(low, high):
    width = low[0][0].shape[2]
    loads, rows, tails = [], [], []
    for group, at in ((low, lambda b: jnp.minimum(b, HALF - 1)), (high, lambda b: jnp.maximum(b - HALF, 0))):
        for array, row in group:
            loads.append(array)
            rows.append(pl.BlockSpec((1, BLK, width), lambda b, row=row, at=at: (row, at(b), 0)))
            tails.append(pl.BlockSpec((1, 16, width), lambda b, row=row: (row, HALF * BLK // 16, 0)))
    return pl.pallas_call(
        mean_kernel,
        out_shape=jax.ShapeDtypeStruct((OWN * BLK, width), BF16),
        grid=(OWN,),
        in_specs=rows + tails,
        out_specs=pl.BlockSpec((BLK, width), lambda b: (b, 0)),
        compiler_params=pltpu.CompilerParams(vmem_limit_bytes=16 << 20),
        name="mean_of",
    )(*loads, *loads)


NARROW = ("y", "x")


def exchanged(copies, axis):
    return lax.all_to_all(copies, axis, split_axis=0, concat_axis=0, tiled=True)


def copied(value, axis):
    count = lax.axis_size(axis) if isinstance(axis, str) else SIDE * SIDE
    return exchanged(jnp.broadcast_to(value, (count, *value.shape)), axis)


def shifted(value, axis, away):
    return lax.ppermute(value, axis, [(k, (k + away) % SIDE) for k in range(SIDE)])


def far_sent(far, axis):
    return shifted(far[0:1], axis, 1), shifted(far[1:2], axis, -1)


def near_sent(near, far_low, far_high, axis):
    plain_high = shifted(near[2:3], axis, 1)
    plain_low = shifted(near[3:4], axis, -1)
    sum_low = shifted(added(far_low, near[0:1]), axis, 1)
    sum_high = shifted(added(far_high, near[1:2]), axis, -1)
    low = [(near, 4), (plain_low, 0), (sum_low, 0)]
    high = [(near, 5), (plain_high, 0), (sum_high, 0)]
    return low, high


def beside_core(value):
    return lax.ppermute(value, "wide", [(k, k ^ 1) for k in range(2 * SIDE)])


def along_z(value, away):
    ring = [(k, (k // 2 + away) % SIDE * 2 + k % 2) for k in range(2 * SIDE)]
    return lax.ppermute(value, "wide", ring)


def square_norms(rows):
    return jnp.sum(jnp.square(rows.astype(F32)), axis=-1)


def body(
    sources,
    targets,
    target_lists,
    target_clusters,
    centroids_src,
    centroids_tgt,
    sender_mean_measure,
    recipient_mean_measure,
):
    width = sources.shape[1]
    wide = lax.axis_size("wide")
    narrow = SIDE * SIDE
    scale = 1.0 / (width * HEAT)
    y, x = lax.axis_index("y"), lax.axis_index("x")
    w = lax.axis_index("wide")
    place = jnp.stack([y, x, w // 2, w % 2]).astype(jnp.int32)

    cols = centroids_tgt.T
    cols = jnp.stack([cols, beside_core(cols)])
    cols = [cols] + [along_z(cols, away) for away in range(1, SIDE)]
    rows = copied(centroids_src, NARROW).reshape(-1, width)

    facts = jnp.concatenate(
        [
            jnp.pad(target_lists.reshape(1, -1).astype(F32), ((0, 0), (0, BLK - OWN * LIST))),
            target_clusters.reshape(OWN, BLK).astype(F32),
            square_norms(sources).reshape(OWN, BLK),
            square_norms(targets).reshape(OWN, BLK),
        ],
        axis=0,
    )
    facts = copied(facts, NARROW).reshape(SIDE, SIDE, LINES, BLK)
    of_column = lax.dynamic_index_in_dim(facts, x, axis=1, keepdims=False)
    of_row = lax.dynamic_index_in_dim(facts, y, axis=0, keepdims=False)
    lists = of_column[:, 0, : OWN * LIST].astype(jnp.int32).reshape(-1)
    ids = of_row[:, 1 : 1 + OWN].astype(jnp.int32).reshape(GROUP, BLK)
    src_sq = of_column[:, 1 + OWN : 1 + 2 * OWN].reshape(GROUP, BLK)
    tgt_sq = of_row[:, 1 + 2 * OWN :].reshape(GROUP, BLK)
    table = entry_table(lists, place)

    rows, sources, targets = lax.optimization_barrier((rows, sources, targets))
    all_targets = lax.all_gather(targets, "x", axis=0).reshape(GROUP, BLK, width)
    all_sources = lax.all_gather(sources, "y", axis=0).reshape(GROUP, BLK, width)

    by_col, by_row = coarse_costs(place, rows, cols, scale)
    row_mass = sender_mean_measure.reshape(-1, BLK)
    col_mass = recipient_mean_measure.reshape(-1, BLK)
    recv = jnp.zeros((wide, *col_mass.shape), F32)
    for turn in range(ITC):
        sent = coarse_half(turn == 0, recv, col_mass, by_row, narrow)
        sent = coarse_half(False, exchanged(sent, NARROW), row_mass, by_col, wide)
        recv = exchanged(sent, "wide")
        if turn == ITC - 3:
            recv, table = lax.optimization_barrier((recv, table))
        if turn == ITC - 2:
            a, at = fine_costs(table, all_sources, all_targets, src_sq, tgt_sq, scale)
            recv, a, at = lax.optimization_barrier((recv, a, at))
    coarse = exchanged(coarse_end(recv, col_mass, narrow), NARROW).reshape(-1, BLK)

    given, first = (coarse, ids), True
    for step in range(STEPS):
        src_parts = exchanged(fine_half(first, AT_TGT, AT_SRC, table, given, at), "y")
        tgt_parts = exchanged(fine_half(False, AT_SRC, AT_TGT, table, (src_parts,), a), "x")
        given, first = (tgt_parts,), False

    s_pot, t_pot, s_own, t_own = final_potentials(place, src_parts, tgt_parts)
    src_args = (table, place, s_pot, t_pot, a, all_targets)
    tgt_args = (table, place, t_pot, s_pot, at, all_sources)
    src_far = far_sent(weighted_sums(True, FAR, *src_args), "y")
    tgt_far = far_sent(weighted_sums(False, FAR, *tgt_args), "x")
    src_near = weighted_sums(True, NEAR, *src_args)
    tgt_near = weighted_sums(False, NEAR, *tgt_args)
    src_mean = mean_of(*near_sent(src_near, *src_far, "y"))
    tgt_mean = mean_of(*near_sent(tgt_near, *tgt_far, "x"))
    return src_mean, tgt_mean, s_own.reshape(-1), t_own.reshape(-1)


def solution(mesh):
    wide, narrow = (mesh.shape[axis] for axis in ("wide", "narrow"))
    devices = mesh.devices.reshape(wide, SIDE, narrow // SIDE)
    grid = Mesh(devices, ("wide", "y", "x"))
    everyone = ("wide", "y", "x")
    in_specs = (
        P(everyone, None),
        P(everyone, None),
        P(everyone, None),
        P(everyone),
        P(everyone, None),
        P(NARROW, "wide"),
        P("wide"),
        P(NARROW),
    )
    out_specs = (P(everyone, None), P(everyone, None), P(everyone), P(everyone))
    return jax.shard_map(body, mesh=grid, in_specs=in_specs, out_specs=out_specs, check_vma=False)
```

time: 685 us -> 387 us (0.56)
  waiting for transfers between devices: 317 us -> 111 us
  Pallas kernels: 0 us -> 80.5 us
  other arithmetic: 66.4 us -> 3.69 us
  local copies, waits for them, and re-layouts: 73.5 us -> 16.7 us
  blocking collectives: 134 us -> 99.1 us
  matrix products: 27.3 us -> 0 us
  between operations: 1.36 us -> 14.5 us
    all_to_all x14 -> x12, waiting for transfers between devices: 317 us -> 64.7 us  [exchanged(): return lax.all_to_all(copies, axis, split_axis=0, concat_axis=0, tiled=True)]
    pallas_call x0 -> x33, Pallas kernels: none -> 80.5 us  [the longest x12 19 us: coarse_half(): pl.pallas_call(functools.partial(coarse_half_kernel, first), out_shape=ja...]
    ppermute x0 -> x16, waiting for transfers between devices: none -> 46.1 us  [the longest x12 34 us: shifted(): lax.ppermute(value, axis, [(k, (k + away) % SIDE) for k in range(SIDE)])]
    all_to_all x12 -> x9, blocking collectives: 134 us -> 99.1 us  [exchanged(): return lax.all_to_all(copies, axis, split_axis=0, concat_axis=0, tiled=True)]
    reduce_max x20 -> x0, other arithmetic: 30.5 us -> none  [the longest x6 12.1 us: lateral_lse_offset(): best_rating = jnp.max(rating_grid_form, axis=1)]
    dot_general x6 -> x0, matrix products: 27.3 us -> none  [the longest x1 10.5 us: body(): jnp.dot(picker, numerator.reshape(slot_count, BLK * feature_count), prefe...]
    scatter x9 -> x0, local copies, waits for them, and re-layouts: 25.4 us -> none  [the longest x8 24.7 us: into_slots(): jnp.zeros((slot_count,) + values.shape[1:], values.dtype).at[slot_of]]
    gather x11 -> x0, local copies, waits for them, and re-layouts: 24.3 us -> none  [the longest x1 7.22 us: body(): jnp.take(received.reshape(slot_count, BLK, feature_count), slot_of, axis=0)]
  transfers between devices with their start and end apart: 14 -> 30, of which waited for: 12 -> 21; matrix products, arithmetic and copies ran while one was open for 8% -> 2% of each run, Pallas kernels for 0% -> 14%
where the time goes in v1:
time: 387 us; the launch traced here: 385 us
  waiting for transfers between devices  111 us (29%)
  blocking collectives  99.1 us (26%)
  Pallas kernels  80.5 us (21%)
  starting transfers between devices  58.8 us (15%)
  local copies, waits for them, and re-layouts  16.7 us (4%)
  between operations  14.5 us (4%)
    all_to_all x9, blocking collectives, exchanged(): return lax.all_to_all(copies, axis, split_axis=0, concat_axis=0, tiled=True)  99.1 us
    all_to_all x12, waiting for transfers between devices, exchanged(): return lax.all_to_all(copies, axis, split_axis=0, concat_axis=0, tiled=True)  64.7 us
    all_to_all x12, starting transfers between devices, exchanged(): return lax.all_to_all(copies, axis, split_axis=0, concat_axis=0, tiled=True)  42.8 us
    ppermute x12, waiting for transfers between devices, shifted(): lax.ppermute(value, axis, [(k, (k + away) % SIDE) for k in range(SIDE)])  34 us
    pallas_call x12, Pallas kernels, coarse_half(): pl.pallas_call(functools.partial(coarse_half_kernel, first), out_shape=ja...  19 us
    pallas_call x4, Pallas kernels, weighted_sums(): pl.pallas_call(functools.partial(sums_kernel, by_src), out_shape=jax.Shap...  16.6 us
    pallas_call x6, Pallas kernels, fine_half(): pl.pallas_call(functools.partial(fine_half_kernel, first, given_at, into_...  14.5 us
    unnamed x50, local copies, waits for them, and re-layouts  12.7 us
  transfers between devices with their start and end apart: 30, of which 21 were waited for; matrix products, arithmetic and copies ran while one was open for 2% of the time, Pallas kernels for 14%

profile of v1, /device:TPU:0, one launch (start us, length us, event | category | flops | bytes accessed | tf_op | source)
XLA Modules:
  0.0 384.8 jit_solution(18327043284372199172)
XLA Ops:
  8.3 29.8 %all_to_all.105 = bf16[16,64,768]{2,1,0:T(8,128)(2,1)} all-to-all(bf16[16,64,768]{2,1,0:T(8,128)(2,1)S(1)} %broadcast_in_dim.10), channel_id=1, replica_groups=mesh['wide'=8,'y'=4,'x'=4] {'y','x'}, dimensions={0} | all-to-all | bytes 3145728 | tf_op jit(solution)/shard_map/all_to_all | solution.py:495
  40.3 4.1 %collective-permute-start.3 = (bf16[2,96,512]{2,1,0:T(8,128)(2,1)S(1)}, bf16[2,96,512]{2,1,0:T(8,128)(2,1)S(1)}, u32[]{:S(2)}, u32[]{:S(2)}) collective-permute-start(bf16[2,96,512]{2,1,0:T(8,128)(2,1)S(1)} %pad_maximum_fusion.refs_0_), channel_id=1, source_target_pairs={{0,96},{16,112},{32,0},{48,16},{64,32},{80,48},{96,64},{112,80},{1... | collective-permute-start | bytes 589832 | tf_op jit(solution)/shard_map/ppermute | solution.py:527
  45.7 7.3 %collective-permute-done.3.refs_3_ = bf16[2,96,512]{2,1,0:T(8,128)(2,1)S(1)} collective-permute-done((bf16[2,96,512]{2,1,0:T(8,128)(2,1)S(1)}, bf16[2,96,512]{2,1,0:T(8,128)(2,1)S(1)}, u32[]{:S(2)}, u32[]{:S(2)}) %collective-permute-start.3) | collective-permute-done | bytes 196640 | tf_op jit(solution)/shard_map/ppermute | solution.py:527
  67.8 7.6 %all-to-all-done.1.recv_ref = f32[16,8,128]{2,1,0:T(8,128)S(1)} async-done(((f32[16,8,128]{2,1,0:T(8,128)}), f32[16,8,128]{2,1,0:T(8,128)S(1)}, u32[]{:S(2)}, u32[]{:S(2)}) %all-to-all-start.1) | async-done | bytes 65568 | tf_op jit(solution)/shard_map/all_to_all | solution.py:495
  94.5 5.7 %all-to-all-done.3.recv_ref = f32[16,8,128]{2,1,0:T(8,128)S(1)} async-done(((f32[16,8,128]{2,1,0:T(8,128)}), f32[16,8,128]{2,1,0:T(8,128)S(1)}, u32[]{:S(2)}, u32[]{:S(2)}) %all-to-all-start.3) | async-done | bytes 65568 | tf_op jit(solution)/shard_map/all_to_all | solution.py:495
  105.2 5.3 %all-to-all-done.4.recv_ref = f32[8,4,128]{2,1,0:T(4,128)S(1)} async-done(((f32[8,4,128]{2,1,0:T(4,128)}), f32[8,4,128]{2,1,0:T(4,128)S(1)}, u32[]{:S(2)}, u32[]{:S(2)}) %all-to-all-start.4) | async-done | bytes 16416 | tf_op jit(solution)/shard_map/all_to_all | solution.py:495
  118.3 5.9 %all-to-all-done.9 = f32[16,25,128]{2,1,0:T(8,128)S(1)} async-done(((f32[16,25,128]{2,1,0:T(8,128)}), f32[16,25,128]{2,1,0:T(8,128)S(1)}, u32[]{:S(2)}, u32[]{:S(2)}) %all-to-all-start.9) | async-done | bytes 204832 | tf_op jit(solution)/shard_map/all_to_all | solution.py:495
  127.9 8.3 %all-to-all-done.5.recv_ref = f32[16,8,128]{2,1,0:T(8,128)S(1)} async-done(((f32[16,8,128]{2,1,0:T(8,128)}), f32[16,8,128]{2,1,0:T(8,128)S(1)}, u32[]{:S(2)}, u32[]{:S(2)}) %all-to-all-start.5) | async-done | bytes 65568 | tf_op jit(solution)/shard_map/all_to_all | solution.py:495
  141.3 5.2 %all-to-all-done.6.recv_ref = f32[8,4,128]{2,1,0:T(4,128)S(1)} async-done(((f32[8,4,128]{2,1,0:T(4,128)}), f32[8,4,128]{2,1,0:T(4,128)S(1)}, u32[]{:S(2)}, u32[]{:S(2)}) %all-to-all-start.6) | async-done | bytes 16416 | tf_op jit(solution)/shard_map/all_to_all | solution.py:495
  153.3 8.3 %all-to-all-done.7.recv_ref = f32[16,8,128]{2,1,0:T(8,128)S(1)} async-done(((f32[16,8,128]{2,1,0:T(8,128)}), f32[16,8,128]{2,1,0:T(8,128)S(1)}, u32[]{:S(2)}, u32[]{:S(2)}) %all-to-all-start.7) | async-done | bytes 65568 | tf_op jit(solution)/shard_map/all_to_all | solution.py:495
  167.3 4.6 %entry_table.1.table_ref.refs_0_ = s32[768]{0:T(1024)} custom-call(s32[128]{0:T(128)} %convert_element_type.45.lists_ref, s32[4]{0:T(128)} %copy-done.14), custom_call_target="tpu_custom_call" | custom-call | tf_op jit(solution)/shard_map/entry_table/pallas_call | solution.py:215
  178.8 7.6 %all-to-all-done.10.recv_ref = f32[16,8,128]{2,1,0:T(8,128)S(1)} async-done(((f32[16,8,128]{2,1,0:T(8,128)}), f32[16,8,128]{2,1,0:T(8,128)S(1)}, u32[]{:S(2)}, u32[]{:S(2)}) %all-to-all-start.10) | async-done | bytes 65568 | tf_op jit(solution)/shard_map/all_to_all | solution.py:495
  188.1 4.7 %all-to-all-start.11 = ((f32[8,4,128]{2,1,0:T(4,128)}), f32[8,4,128]{2,1,0:T(4,128)S(1)}, u32[]{:S(2)}, u32[]{:S(2)}) async-start(f32[8,4,128]{2,1,0:T(4,128)} %coarse_half.21), calls=%async_computation.11 | async-start | bytes 32768 | tf_op jit(solution)/shard_map/all_to_all | solution.py:495
  193.4 11.6 %fine_costs.1 = (f32[52,128,128]{2,1,0:T(8,128)}, f32[52,128,128]{2,1,0:T(8,128)}) custom-call(s32[768]{0:T(1024)} %entry_table.1.table_ref.refs_0_, bf16[32,128,768]{2,1,0:T(8,128)(2,1)} %bitcast.32, bf16[32,128,768]{2,1,0:T(8,128)(2,1)} %bitcast.37, f32[32,128]{1,0:T(8,128)} %get-tuple-element.51.xsq_ref, f32[32,128]{1,0:T(8,128)} %get-tuple-element.50.ysq_ref), custom_call_target="tpu_custom_call" | custom-call | tf_op jit(solution)/shard_map/fine_costs/pallas_call | solution.py:245
  207.7 11.3 %all_to_all.106.recv_ref = f32[16,8,128]{2,1,0:T(8,128)S(1)} all-to-all(f32[16,8,128]{2,1,0:T(8,128)S(1)} %coarse_half.22), channel_id=1, replica_groups=mesh['wide'=8,'y'=4,'x'=4] {'y','x'}, dimensions={0} | all-to-all | bytes 131072 | tf_op jit(solution)/shard_map/all_to_all | solution.py:495
  221.6 10.0 %all_to_all.107.recv_ref = f32[8,4,128]{2,1,0:T(4,128)} all-to-all(f32[8,4,128]{2,1,0:T(4,128)S(1)} %coarse_half.23), channel_id=1, replica_groups=mesh['wide'=8,'y'=4,'x'=4] {'wide'}, dimensions={0} | all-to-all | bytes 32768 | tf_op jit(solution)/shard_map/all_to_all | solution.py:495
  233.0 3.7 all-to-all-start.14
  236.7 7.3 %all-to-all-done.14 = f32[16,4,128]{2,1,0:T(4,128)S(1)} async-done(((f32[16,4,128]{2,1,0:T(4,128)}), f32[16,4,128]{2,1,0:T(4,128)S(1)}, u32[]{:S(2)}, u32[]{:S(2)}) %all-to-all-start.14) | async-done | bytes 32800 | tf_op jit(solution)/shard_map/all_to_all | solution.py:495
  244.0 4.1 %fine_half.6 = f32[4,32,128]{2,1,0:T(8,128)S(1)} custom-call(s32[768]{0:T(1024)S(1)} %copy-done.11, f32[64,128]{1,0:T(8,128)S(1)} %bitcast.49, s32[32,128]{1,0:T(8,128)S(1)} %fusion.2.refs_2_, f32[52,128,128]{2,1,0:T(8,128)S(1)} %copy-done), custom_call_target="tpu_custom_call" | custom-call | tf_op jit(solution)/shard_map/fine_half/pallas_call | solution.py:319
  248.1 8.0 %all_to_all.108.refs_1_ = f32[4,32,128]{2,1,0:T(8,128)S(1)} all-to-all(f32[4,32,128]{2,1,0:T(8,128)S(1)} %fine_half.6), channel_id=1, replica_groups=mesh['wide'=8,'y'=4,'x'=4] {'y'}, dimensions={0} | all-to-all | bytes 131072 | tf_op jit(solution)/shard_map/all_to_all | solution.py:495
  258.2 8.0 %all_to_all.109.refs_1_ = f32[4,32,128]{2,1,0:T(8,128)S(1)} all-to-all(f32[4,32,128]{2,1,0:T(8,128)S(1)} %fine_half.7), channel_id=1, replica_groups=mesh['wide'=8,'y'=4,'x'=4] {'x'}, dimensions={0} | all-to-all | bytes 131072 | tf_op jit(solution)/shard_map/all_to_all | solution.py:495
  268.3 8.0 %all_to_all.110.refs_1_ = f32[4,32,128]{2,1,0:T(8,128)S(1)} all-to-all(f32[4,32,128]{2,1,0:T(8,128)S(1)} %fine_half.8), channel_id=1, replica_groups=mesh['wide'=8,'y'=4,'x'=4] {'y'}, dimensions={0} | all-to-all | bytes 131072 | tf_op jit(solution)/shard_map/all_to_all | solution.py:495
  278.4 8.0 %all_to_all.111.refs_1_ = f32[4,32,128]{2,1,0:T(8,128)S(1)} all-to-all(f32[4,32,128]{2,1,0:T(8,128)S(1)} %fine_half.9), channel_id=1, replica_groups=mesh['wide'=8,'y'=4,'x'=4] {'x'}, dimensions={0} | all-to-all | bytes 131072 | tf_op jit(solution)/shard_map/all_to_all | solution.py:495
  288.6 8.0 %all_to_all.112.refs_1_.srecv_ref = f32[4,32,128]{2,1,0:T(8,128)S(1)} all-to-all(f32[4,32,128]{2,1,0:T(8,128)S(1)} %fine_half.10), channel_id=1, replica_groups=mesh['wide'=8,'y'=4,'x'=4] {'y'}, dimensions={0} | all-to-all | bytes 131072 | tf_op jit(solution)/shard_map/all_to_all | solution.py:495
  298.7 8.0 %all_to_all.113.trecv_ref = f32[4,32,128]{2,1,0:T(8,128)S(1)} all-to-all(f32[4,32,128]{2,1,0:T(8,128)S(1)} %fine_half.11), channel_id=1, replica_groups=mesh['wide'=8,'y'=4,'x'=4] {'x'}, dimensions={0} | all-to-all | bytes 131072 | tf_op jit(solution)/shard_map/all_to_all | solution.py:495
  317.2 6.0 %weighted_sums.4.refs_0_.refs_3_.refs_6_.refs_9_ = bf16[6,528,768]{2,1,0:T(8,128)(2,1)S(1)} custom-call(s32[768]{0:T(1024)S(1)} %copy-done.11, s32[4]{0:T(128)S(1)} %copy-done.15, s32[6]{0:T(128)S(1)} %copy-done.16, f32[32,128]{1,0:T(8,128)S(1)} %get-tuple-element.32.mine_ref.other_ref, f32[32,128]{1,0:T(8,128)S(1)} %get-tuple-element.33.other_ref.mine_ref, ...), custom_call_target="tpu_custom_call" | custom-call | tf_op jit(solution)/shard_map/weighted_sums/pallas_call | solution.py:416
  331.0 5.7 %weighted_sums.6.refs_0_.refs_3_.refs_6_.refs_9_ = bf16[6,528,768]{2,1,0:T(8,128)(2,1)S(1)} custom-call(s32[768]{0:T(1024)S(1)} %copy-done.11, s32[4]{0:T(128)S(1)} %copy-done.15, s32[6]{0:T(128)S(1)} %copy-done.16, f32[32,128]{1,0:T(8,128)S(1)} %get-tuple-element.33.other_ref.mine_ref, f32[32,128]{1,0:T(8,128)S(1)} %get-tuple-element.32.mine_ref.other_ref, ...), custom_call_target="tpu_custom_call" | custom-call | tf_op jit(solution)/shard_map/weighted_sums/pallas_call | solution.py:416
  340.8 7.6 %collective-permute-done.7.refs_4_.refs_10_ = bf16[1,528,768]{2,1,0:T(8,128)(2,1)S(1)} collective-permute-done((bf16[1,528,768]{2,1,0:T(8,128)(2,1)S(1)}, bf16[1,528,768]{2,1,0:T(8,128)(2,1)S(1)}, u32[]{:S(2)}, u32[]{:S(2)}) %collective-permute-start.7) | collective-permute-done | bytes 811040 | tf_op jit(solution)/shard_map/ppermute | solution.py:504
  349.4 8.2 %collective-permute-done.9.refs_5_.refs_11_ = bf16[1,528,768]{2,1,0:T(8,128)(2,1)S(1)} collective-permute-done((bf16[1,528,768]{2,1,0:T(8,128)(2,1)S(1)}, bf16[1,528,768]{2,1,0:T(8,128)(2,1)S(1)}, u32[]{:S(2)}, u32[]{:S(2)}) %collective-permute-start.9) | collective-permute-done | bytes 811040 | tf_op jit(solution)/shard_map/ppermute | solution.py:504
  359.9 3.7 mean_of.2
  365.5 8.7 %collective-permute-done.15.refs_5_.refs_11_ = bf16[1,528,768]{2,1,0:T(8,128)(2,1)S(1)} collective-permute-done((bf16[1,528,768]{2,1,0:T(8,128)(2,1)S(1)}, bf16[1,528,768]{2,1,0:T(8,128)(2,1)S(1)}, u32[]{:S(2)}, u32[]{:S(2)}) %collective-permute-start.15) | collective-permute-done | bytes 811040 | tf_op jit(solution)/shard_map/ppermute | solution.py:504
  374.2 3.7 mean_of.3
  (149 shorter events, 126.2 us)
Async XLA Ops:
  7.2 186.2 %all-gather.5.cloned.1.call-start = ((), (), s32[]{:S(2)}) async-start(), calls=%async_computation.21 | async-start | bytes 7864320 | tf_op jit(solution)/shard_map/all_gather | solution.py:577
  38.1 155.3 %all-gather.7.cloned.1.call-start = ((), (), s32[]{:S(2)}) async-start(), calls=%async_computation.22 | async-start | bytes 7864320 | tf_op jit(solution)/shard_map/all_gather | solution.py:576
  39.0 1.3 collective-permute-start
  40.3 12.8 %collective-permute-start.3 = (bf16[2,96,512]{2,1,0:T(8,128)(2,1)S(1)}, bf16[2,96,512]{2,1,0:T(8,128)(2,1)S(1)}, u32[]{:S(2)}, u32[]{:S(2)}) collective-permute-start(bf16[2,96,512]{2,1,0:T(8,128)(2,1)S(1)} %pad_maximum_fusion.refs_0_), channel_id=1, source_target_pairs={{0,96},{16,112},{32,0},{48,16},{64,32},{80,48},{96,64},{112,80},{1... | collective-permute-start | bytes 589832 | tf_op jit(solution)/shard_map/ppermute | solution.py:527
  44.4 9.3 %collective-permute-start.2 = (bf16[2,96,512]{2,1,0:T(8,128)(2,1)S(1)}, bf16[2,96,512]{2,1,0:T(8,128)(2,1)S(1)}, u32[]{:S(2)}, u32[]{:S(2)}) collective-permute-start(bf16[2,96,512]{2,1,0:T(8,128)(2,1)S(1)} %pad_maximum_fusion.refs_0_), channel_id=1, source_target_pairs={{0,64},{16,80},{32,96},{48,112},{64,0},{80,16},{96,32},{112,48},{1... | collective-permute-start | bytes 589832 | tf_op jit(solution)/shard_map/ppermute | solution.py:527
  44.4 12.1 %collective-permute-start.1 = (bf16[2,96,512]{2,1,0:T(8,128)(2,1)S(1)}, bf16[2,96,512]{2,1,0:T(8,128)(2,1)S(1)}, u32[]{:S(2)}, u32[]{:S(2)}) collective-permute-start(bf16[2,96,512]{2,1,0:T(8,128)(2,1)S(1)} %pad_maximum_fusion.refs_0_), channel_id=1, source_target_pairs={{0,32},{16,48},{32,64},{48,80},{64,96},{80,112},{96,0},{112,16},{1... | collective-permute-start | bytes 589832 | tf_op jit(solution)/shard_map/ppermute | solution.py:527
  61.4 125.0 %copy-start.2 = (f32[4,1024,128]{2,1,0:T(8,128)}, f32[4,1024,128]{2,1,0:T(8,128)S(1)}, u32[]{:S(2)}) copy-start(f32[4,1024,128]{2,1,0:T(8,128)S(1)} %get-tuple-element.22.cost_ref) | copy-start | bytes 6291460
  64.3 11.1 %all-to-all-start.1 = ((f32[16,8,128]{2,1,0:T(8,128)}), f32[16,8,128]{2,1,0:T(8,128)S(1)}, u32[]{:S(2)}, u32[]{:S(2)}) async-start(f32[16,8,128]{2,1,0:T(8,128)} %coarse_half.12), calls=%async_computation.1 | async-start | bytes 131072 | tf_op jit(solution)/shard_map/all_to_all | solution.py:495
  77.1 8.6 %all-to-all-start.2 = ((f32[8,4,128]{2,1,0:T(4,128)}), f32[8,4,128]{2,1,0:T(4,128)S(1)}, u32[]{:S(2)}, u32[]{:S(2)}) async-start(f32[8,4,128]{2,1,0:T(4,128)} %coarse_half.13), calls=%async_computation.2 | async-start | bytes 32768 | tf_op jit(solution)/shard_map/all_to_all | solution.py:495
  89.0 11.2 %all-to-all-start.3 = ((f32[16,8,128]{2,1,0:T(8,128)}), f32[16,8,128]{2,1,0:T(8,128)S(1)}, u32[]{:S(2)}, u32[]{:S(2)}) async-start(f32[16,8,128]{2,1,0:T(8,128)} %coarse_half.14), calls=%async_computation.3 | async-start | bytes 131072 | tf_op jit(solution)/shard_map/all_to_all | solution.py:495
  101.9 8.6 %all-to-all-start.4 = ((f32[8,4,128]{2,1,0:T(4,128)}), f32[8,4,128]{2,1,0:T(4,128)S(1)}, u32[]{:S(2)}, u32[]{:S(2)}) async-start(f32[8,4,128]{2,1,0:T(4,128)} %coarse_half.15), calls=%async_computation.4 | async-start | bytes 32768 | tf_op jit(solution)/shard_map/all_to_all | solution.py:495
  111.2 13.0 %all-to-all-start.9 = ((f32[16,25,128]{2,1,0:T(8,128)}), f32[16,25,128]{2,1,0:T(8,128)S(1)}, u32[]{:S(2)}, u32[]{:S(2)}) async-start(f32[16,25,128]{2,1,0:T(8,128)} %broadcast_in_dim.11), calls=%async_computation.9 | async-start | bytes 524288 | tf_op jit(solution)/shard_map/all_to_all | solution.py:495
  124.2 11.9 %all-to-all-start.5 = ((f32[16,8,128]{2,1,0:T(8,128)}), f32[16,8,128]{2,1,0:T(8,128)S(1)}, u32[]{:S(2)}, u32[]{:S(2)}) async-start(f32[16,8,128]{2,1,0:T(8,128)} %coarse_half.16), calls=%async_computation.5 | async-start | bytes 131072 | tf_op jit(solution)/shard_map/all_to_all | solution.py:495
  137.9 8.6 %all-to-all-start.6 = ((f32[8,4,128]{2,1,0:T(4,128)}), f32[8,4,128]{2,1,0:T(4,128)S(1)}, u32[]{:S(2)}, u32[]{:S(2)}) async-start(f32[8,4,128]{2,1,0:T(4,128)} %coarse_half.17), calls=%async_computation.6 | async-start | bytes 32768 | tf_op jit(solution)/shard_map/all_to_all | solution.py:495
  149.8 11.8 %all-to-all-start.7 = ((f32[16,8,128]{2,1,0:T(8,128)}), f32[16,8,128]{2,1,0:T(8,128)S(1)}, u32[]{:S(2)}, u32[]{:S(2)}) async-start(f32[16,8,128]{2,1,0:T(8,128)} %coarse_half.18), calls=%async_computation.7 | async-start | bytes 131072 | tf_op jit(solution)/shard_map/all_to_all | solution.py:495
  163.3 8.6 %all-to-all-start.8 = ((f32[8,4,128]{2,1,0:T(4,128)}), f32[8,4,128]{2,1,0:T(4,128)S(1)}, u32[]{:S(2)}, u32[]{:S(2)}) async-start(f32[8,4,128]{2,1,0:T(4,128)} %coarse_half.19), calls=%async_computation.8 | async-start | bytes 32768 | tf_op jit(solution)/shard_map/all_to_all | solution.py:495
  175.3 11.1 %all-to-all-start.10 = ((f32[16,8,128]{2,1,0:T(8,128)}), f32[16,8,128]{2,1,0:T(8,128)S(1)}, u32[]{:S(2)}, u32[]{:S(2)}) async-start(f32[16,8,128]{2,1,0:T(8,128)} %coarse_half.20), calls=%async_computation.10 | async-start | bytes 131072 | tf_op jit(solution)/shard_map/all_to_all | solution.py:495
  188.1 17.0 %all-to-all-start.11 = ((f32[8,4,128]{2,1,0:T(4,128)}), f32[8,4,128]{2,1,0:T(4,128)S(1)}, u32[]{:S(2)}, u32[]{:S(2)}) async-start(f32[8,4,128]{2,1,0:T(4,128)} %coarse_half.21), calls=%async_computation.11 | async-start | bytes 32768 | tf_op jit(solution)/shard_map/all_to_all | solution.py:495
  233.0 11.0 %all-to-all-start.14 = ((f32[16,4,128]{2,1,0:T(4,128)}), f32[16,4,128]{2,1,0:T(4,128)S(1)}, u32[]{:S(2)}, u32[]{:S(2)}) async-start(f32[16,4,128]{2,1,0:T(4,128)} %coarse_end.1), calls=%async_computation.14 | async-start | bytes 65536 | tf_op jit(solution)/shard_map/all_to_all | solution.py:495
  256.1 51.7 %slice-start.2 = ((s8[6291456]{0:T(1024)(128)(4,1)}), s8[4194304]{0:T(1024)(128)(4,1)S(1)}, s32[]{:S(2)}) async-start(s8[6291456]{0:T(1024)(128)(4,1)} %bitcast.38), calls=%async_computation.25 | async-start | bytes 8388608
  310.0 17.9 %collective-permute-start.8 = (bf16[1,528,768]{2,1,0:T(8,128)(2,1)S(1)}, bf16[1,528,768]{2,1,0:T(8,128)(2,1)S(1)}, u32[]{:S(2)}, u32[]{:S(2)}) collective-permute-start(bf16[1,528,768]{2,1,0:T(8,128)(2,1)S(1)} %get-tuple-element.46), channel_id=1, source_target_pairs={{0,12},{4,0},{8,4},{12,8},{1,13},{5,1},{9,5},{13,9},{2,14},{6,2},{... | collective-permute-start | bytes 2433032 | tf_op jit(solution)/shard_map/ppermute | solution.py:504
  311.7 19.4 %collective-permute-start.5 = (bf16[1,528,768]{2,1,0:T(8,128)(2,1)S(1)}, bf16[1,528,768]{2,1,0:T(8,128)(2,1)S(1)}, u32[]{:S(2)}, u32[]{:S(2)}) collective-permute-start(bf16[1,528,768]{2,1,0:T(8,128)(2,1)S(1)} %get-tuple-element.47), channel_id=1, source_target_pairs={{0,4},{4,8},{8,12},{12,0},{1,5},{5,9},{9,13},{13,1},{2,6},{6,10},{... | collective-permute-start | bytes 2433032 | tf_op jit(solution)/shard_map/ppermute | solution.py:504
  315.1 22.9 %collective-permute-start.14 = (bf16[1,528,768]{2,1,0:T(8,128)(2,1)S(1)}, bf16[1,528,768]{2,1,0:T(8,128)(2,1)S(1)}, u32[]{:S(2)}, u32[]{:S(2)}) collective-permute-start(bf16[1,528,768]{2,1,0:T(8,128)(2,1)S(1)} %get-tuple-element.44), channel_id=1, source_target_pairs={{0,3},{1,0},{2,1},{3,2},{4,7},{5,4},{6,5},{7,6},{8,11},{9,8},{10,9... | collective-permute-start | bytes 2433032 | tf_op jit(solution)/shard_map/ppermute | solution.py:504
  316.4 20.8 %collective-permute-start.11 = (bf16[1,528,768]{2,1,0:T(8,128)(2,1)S(1)}, bf16[1,528,768]{2,1,0:T(8,128)(2,1)S(1)}, u32[]{:S(2)}, u32[]{:S(2)}) collective-permute-start(bf16[1,528,768]{2,1,0:T(8,128)(2,1)S(1)} %get-tuple-element.45), channel_id=1, source_target_pairs={{0,1},{1,2},{2,3},{3,0},{4,5},{5,6},{6,7},{7,4},{8,9},{9,10},{10,1... | collective-permute-start | bytes 2433032 | tf_op jit(solution)/shard_map/ppermute | solution.py:504
  323.4 25.0 %collective-permute-start.7 = (bf16[1,528,768]{2,1,0:T(8,128)(2,1)S(1)}, bf16[1,528,768]{2,1,0:T(8,128)(2,1)S(1)}, u32[]{:S(2)}, u32[]{:S(2)}) collective-permute-start(bf16[1,528,768]{2,1,0:T(8,128)(2,1)S(1)} %get-tuple-element.41), channel_id=1, source_target_pairs={{0,4},{4,8},{8,12},{12,0},{1,5},{5,9},{9,13},{13,1},{2,6},{6,10},{... | collective-permute-start | bytes 2433032 | tf_op jit(solution)/shard_map/ppermute | solution.py:504
  328.0 21.4 %collective-permute-start.4 = (bf16[1,528,768]{2,1,0:T(8,128)(2,1)S(1)}, bf16[1,528,768]{2,1,0:T(8,128)(2,1)S(1)}, u32[]{:S(2)}, u32[]{:S(2)}) collective-permute-start(bf16[1,528,768]{2,1,0:T(8,128)(2,1)S(1)} %get-tuple-element.43), channel_id=1, source_target_pairs={{0,12},{4,0},{8,4},{12,8},{1,13},{5,1},{9,5},{13,9},{2,14},{6,2},{... | collective-permute-start | bytes 2433032 | tf_op jit(solution)/shard_map/ppermute | solution.py:504
  331.0 26.5 %collective-permute-start.9 = (bf16[1,528,768]{2,1,0:T(8,128)(2,1)S(1)}, bf16[1,528,768]{2,1,0:T(8,128)(2,1)S(1)}, u32[]{:S(2)}, u32[]{:S(2)}) collective-permute-start(bf16[1,528,768]{2,1,0:T(8,128)(2,1)S(1)} %added.5), channel_id=1, source_target_pairs={{0,12},{4,0},{8,4},{12,8},{1,13},{5,1},{9,5},{13,9},{2,14},{6,2},{... | collective-permute-start | bytes 2433032 | tf_op jit(solution)/shard_map/ppermute | solution.py:504
  337.1 26.4 %collective-permute-start.13 = (bf16[1,528,768]{2,1,0:T(8,128)(2,1)S(1)}, bf16[1,528,768]{2,1,0:T(8,128)(2,1)S(1)}, u32[]{:S(2)}, u32[]{:S(2)}) collective-permute-start(bf16[1,528,768]{2,1,0:T(8,128)(2,1)S(1)} %get-tuple-element.37), channel_id=1, source_target_pairs={{0,1},{1,2},{2,3},{3,0},{4,5},{5,6},{6,7},{7,4},{8,9},{9,10},{10,1... | collective-permute-start | bytes 2433032 | tf_op jit(solution)/shard_map/ppermute | solution.py:504
  338.0 21.9 %collective-permute-start.6 = (bf16[1,528,768]{2,1,0:T(8,128)(2,1)S(1)}, bf16[1,528,768]{2,1,0:T(8,128)(2,1)S(1)}, u32[]{:S(2)}, u32[]{:S(2)}) collective-permute-start(bf16[1,528,768]{2,1,0:T(8,128)(2,1)S(1)} %added.4), channel_id=1, source_target_pairs={{0,4},{4,8},{8,12},{12,0},{1,5},{5,9},{9,13},{13,1},{2,6},{6,10},{... | collective-permute-start | bytes 2433032 | tf_op jit(solution)/shard_map/ppermute | solution.py:504
  348.4 17.1 %collective-permute-start.10 = (bf16[1,528,768]{2,1,0:T(8,128)(2,1)S(1)}, bf16[1,528,768]{2,1,0:T(8,128)(2,1)S(1)}, u32[]{:S(2)}, u32[]{:S(2)}) collective-permute-start(bf16[1,528,768]{2,1,0:T(8,128)(2,1)S(1)} %get-tuple-element.39), channel_id=1, source_target_pairs={{0,3},{1,0},{2,1},{3,2},{4,7},{5,4},{6,5},{7,6},{8,11},{9,8},{10,9... | collective-permute-start | bytes 2433032 | tf_op jit(solution)/shard_map/ppermute | solution.py:504
  349.3 24.9 %collective-permute-start.15 = (bf16[1,528,768]{2,1,0:T(8,128)(2,1)S(1)}, bf16[1,528,768]{2,1,0:T(8,128)(2,1)S(1)}, u32[]{:S(2)}, u32[]{:S(2)}) collective-permute-start(bf16[1,528,768]{2,1,0:T(8,128)(2,1)S(1)} %added.7), channel_id=1, source_target_pairs={{0,3},{1,0},{2,1},{3,2},{4,7},{5,4},{6,5},{7,6},{8,11},{9,8},{10,9... | collective-permute-start | bytes 2433032 | tf_op jit(solution)/shard_map/ppermute | solution.py:504
  357.6 16.7 %collective-permute-start.12 = (bf16[1,528,768]{2,1,0:T(8,128)(2,1)S(1)}, bf16[1,528,768]{2,1,0:T(8,128)(2,1)S(1)}, u32[]{:S(2)}, u32[]{:S(2)}) collective-permute-start(bf16[1,528,768]{2,1,0:T(8,128)(2,1)S(1)} %added.6), channel_id=1, source_target_pairs={{0,1},{1,2},{2,3},{3,0},{4,5},{5,6},{6,7},{7,4},{8,9},{9,10},{10,1... | collective-permute-start | bytes 2433032 | tf_op jit(solution)/shard_map/ppermute | solution.py:504
  (23 other events, 253.2 us)
Sparse Core Ops, SparseCore 0:
  38.2 65.5 all-gather.4
  105.5 67.9 all-gather.6

commit v2 on v1

--- a/solution.py
+++ b/solution.py
@@ -21,8 +21,7 @@
 SLOTS = SIDE * SIDE * CAP + UNROLL
 HALF = OWN // 2
 HALF_ROWS = HALF * BLK + 16
-FAR = (4, 5)
-NEAR = (2, 7, 3, 6, 0, 1)
+FAR, PLAIN, JOINT, HOME = (4, 5), (6, 3), (2, 7), (0, 1)
 NEG = -1e30
 AT_SRC, AT_TGT, AT_START, AT_COUNT, AT_LIST, AT_LIVE, TABLE = 0, 64, 128, 168, 200, 712, 768
 LINES = 3 * OWN + 1
@@ -51,15 +50,10 @@
         col_ref[k] = jnp.broadcast_to(columns[:, k : k + 1], (BLK, BLK))
 
 
-def joined(parts_ref):
-    count = parts_ref.shape[0]
-    top = parts_ref[0]
-    for k in range(1, count):
-        top = jnp.maximum(top, parts_ref[k])
-    total = jnp.exp(parts_ref[0] - top)
-    for k in range(1, count):
-        total = total + jnp.exp(parts_ref[k] - top)
-    return top + jnp.log(total)
+def joined(parts_ref, rows=None):
+    parts = [parts_ref[k, 0:rows, :] for k in range(parts_ref.shape[0])]
+    top = tree(parts, jnp.maximum)
+    return top + jnp.log(tree([jnp.exp(part - top) for part in parts], jnp.add))
 
 
 def tree(parts, op):
@@ -127,7 +121,7 @@
     if first:
         potential = jnp.zeros((given, BLK), F32)
     else:
-        potential = jnp.log(mass_ref[...]) - joined(recv_ref)
+        potential = jnp.log(mass_ref[...]) - joined(recv_ref, given)
     spread(col_ref, columns_of(potential), given)
 
     def chunk(c, carry):
@@ -147,14 +141,17 @@
     lax.fori_loop(0, chunks, chunk, 0)
     result = res_ref[0:chunks, :]
     for k in range(out_ref.shape[0]):
-        out_ref[k] = result
+        out_ref[k, 0:chunks, :] = result
+        if first:
+            out_ref[k, chunks:, :] = recv_ref[...]
 
 
 def coarse_half(first, recv, mass, cost, copies):
     given, chunks = mass.shape[0], cost.shape[0]
+    lines = chunks + (recv.shape[0] if first else 0)
     return pl.pallas_call(
         functools.partial(coarse_half_kernel, first),
-        out_shape=jax.ShapeDtypeStruct((copies, chunks, BLK), F32),
+        out_shape=jax.ShapeDtypeStruct((copies, lines, BLK), F32),
         in_specs=spec(3),
         out_specs=spec(1)[0],
         scratch_shapes=[pltpu.VMEM((given, BLK, BLK), F32), pltpu.VMEM((8, BLK), F32)],
@@ -248,6 +245,7 @@
         in_specs=smem(1) + spec(4),
         out_specs=tuple(spec(2)),
         scratch_shapes=[pltpu.VMEM((GROUP, BLK, BLK), F32)],
+        compiler_params=pltpu.CompilerParams(vmem_limit_bytes=24 << 20),
         name="fine_costs",
     )(table, x, y, xsq, ysq)
 
@@ -277,14 +275,19 @@
     lax.fori_loop(0, GROUP // UNROLL, some, 0)
 
 
-def fine_half_kernel(first, given_at, into_at, *refs):
+def fine_half_kernel(first, last, given_at, into_at, *refs):
+    *refs, col_ref, top_ref, sum_ref = refs
+    if last:
+        *refs, pot_ref = refs
     if first:
-        table_ref, coarse_ref, ids_ref, mat_ref, out_ref, col_ref, top_ref, sum_ref = refs
+        table_ref, coarse_ref, ids_ref, mat_ref, out_ref = refs
         looked_up(coarse_ref, ids_ref, top_ref)
         potential = top_ref[0:GROUP, :]
     else:
-        table_ref, recv_ref, mat_ref, out_ref, col_ref, top_ref, sum_ref = refs
+        table_ref, recv_ref, mat_ref, out_ref = refs
         potential = -joined(recv_ref)
+    if last:
+        pot_ref[...] = potential
     spread(col_ref, columns_of(potential), GROUP)
     top_ref[...] = jnp.full(top_ref.shape, NEG, F32)
     sum_ref[...] = jnp.zeros(sum_ref.shape, F32)
@@ -315,12 +318,16 @@
         out_ref[k] = result
 
 
-def fine_half(first, given_at, into_at, table, given, mat):
-    return pl.pallas_call(
-        functools.partial(fine_half_kernel, first, given_at, into_at),
-        out_shape=jax.ShapeDtypeStruct((SIDE, GROUP, BLK), F32),
+def fine_half(first, last, given_at, into_at, table, given, mat):
+    shapes = (
+        jax.ShapeDtypeStruct((SIDE, GROUP, BLK), F32),
+        jax.ShapeDtypeStruct((GROUP, BLK), F32),
+    )
+    return pl.pallas_call(
+        functools.partial(fine_half_kernel, first, last, given_at, into_at),
+        out_shape=shapes if last else shapes[0],
         in_specs=smem(1) + spec(len(given) + 1),
-        out_specs=spec(1)[0],
+        out_specs=tuple(spec(2)) if last else spec(1)[0],
         scratch_shapes=[
             pltpu.VMEM((GROUP, BLK, BLK), F32),
             pltpu.VMEM((GROUP + 8, BLK), F32),
@@ -331,39 +338,48 @@
     )(table, *given, mat)
 
 
-def own_kernel(place_ref, srecv_ref, trecv_ref, s_ref, t_ref, sown_ref, town_ref):
-    s_ref[...] = -joined(srecv_ref)
+def own_kernel(place_ref, s_ref, trecv_ref, t_ref, sown_ref, town_ref, share_ref):
+    y, x = place_ref[0], place_ref[1]
     t_ref[...] = -joined(trecv_ref)
-    own_s = pl.ds(pl.multiple_of(place_ref[0] * OWN, OWN), OWN)
-    own_t = pl.ds(pl.multiple_of(place_ref[1] * OWN, OWN), OWN)
-    sown_ref[...] = HEAT * s_ref[own_s, :]
-    town_ref[...] = HEAT * t_ref[own_t, :]
-
-
-def final_potentials(place, srecv, trecv):
+
+    def owned(device):
+        return pl.ds(pl.multiple_of(device * OWN, OWN), OWN)
+
+    sown_ref[...] = HEAT * s_ref[owned(y), :]
+    town_ref[...] = HEAT * t_ref[owned(x), :]
+    after, before = lax.rem(x + 1, SIDE), lax.rem(x + SIDE - 1, SIDE)
+    for k, (sender, owner) in enumerate(((before, after), (after, before))):
+        share = jnp.exp(trecv_ref[sender, owned(owner), :] + t_ref[owned(owner), :])
+        share_ref[k, 0:HALF, :] = share[k * HALF : (k + 1) * HALF, :]
+        share_ref[k, HALF:, :] = jnp.zeros((OWN - HALF, BLK), F32)
+
+
+def final_potentials(place, s_pot, trecv):
     some = jax.ShapeDtypeStruct((GROUP, BLK), F32)
     own = jax.ShapeDtypeStruct((OWN, BLK), F32)
     return pl.pallas_call(
         own_kernel,
-        out_shape=(some, some, own, own),
+        out_shape=(some, own, own, jax.ShapeDtypeStruct((2, OWN, BLK), F32)),
         in_specs=smem(1) + spec(2),
         out_specs=tuple(spec(4)),
         compiler_params=pltpu.CompilerParams(vmem_limit_bytes=4 << 20),
         name="final_potentials",
-    )(place, srecv, trecv)
-
-
-def masses_put(buf, at, mass, width):
+    )(place, s_pot, trecv)
+
+
+def masses_put(buf, mass):
+    width = buf.shape[1]
     high = mass.astype(BF16).astype(F32)
     both = jnp.concatenate([high, mass - high, jnp.zeros((8, width - 2 * BLK), F32)], axis=1)
-    buf[at, HALF * BLK :, :] = jnp.concatenate([both, jnp.zeros_like(both)], axis=0).astype(BF16)
+    buf[HALF * BLK :, :] = jnp.concatenate([both, jnp.zeros_like(both)], axis=0).astype(BF16)
 
 
 def masses_of(tail):
     return tail[:, 0:BLK].astype(F32) + tail[:, BLK : 2 * BLK].astype(F32)
 
 
-def sums_kernel(by_src, table_ref, place_ref, picks_ref, mine_ref, other_ref, mat_ref, rows_ref, out_ref, acc_ref, mass_ref):
+def sums_kernel(by_src, table_ref, place_ref, picks_ref, mine_ref, other_ref, mat_ref, rows_ref, *refs):
+    *out_refs, acc_ref, mass_ref = refs
     q = pl.program_id(0)
     away, half = lax.div(picks_ref[q], 2), lax.rem(picks_ref[q], 2)
     base = lax.rem(place_ref[0 if by_src else 1] + away, SIDE) * OWN + half * HALF
@@ -384,65 +400,81 @@
         mass = lax.dot_general(ones, plan, (((1,), (1,)), ((), ())), preferred_element_type=F32)
         return total, mass[0:1, :]
 
-    columns, counts = [], []
+    def column_of(block):
+        if len(mine_ref.shape) == 3:
+            line = -mine_ref[0, pl.ds(block, 1), :]
+        else:
+            line = mine_ref[pl.ds(block, 1), :]
+        return jnp.broadcast_to(line, (BLK, BLK)).T
+
+    counts = []
     for b in range(HALF):
         block = base + b
         if by_src:
             count = table_ref[AT_START + block + 1] - table_ref[AT_START + block]
         else:
             count = table_ref[AT_COUNT + block]
-        column = jnp.broadcast_to(mine_ref[pl.ds(block, 1), :], (BLK, BLK)).T
-        total, mass = term(block, 0, column, count > 0)
+        total, mass = term(block, 0, column_of(block), count > 0)
         acc_ref[b] = total
         mass_ref[b : b + 1, :] = mass
         counts.append(count)
     for b in range(HALF):
 
         def more(k, carry, b=b):
-            column = jnp.broadcast_to(mine_ref[pl.ds(base + b, 1), :], (BLK, BLK)).T
-            total, mass = term(base + b, k, column, None)
+            total, mass = term(base + b, k, column_of(base + b), None)
             acc_ref[b] += total
             mass_ref[b : b + 1, :] += mass
             return carry
 
         lax.fori_loop(1, counts[b], more, 0)
-    for b in range(HALF):
-        out_ref[0, b * BLK : (b + 1) * BLK, :] = acc_ref[b].astype(BF16)
-    masses_put(out_ref, 0, mass_ref[...], out_ref.shape[2])
+    for k, out_ref in enumerate(out_refs):
+
+        @pl.when(q == k)
+        def _(out_ref=out_ref):
+            for b in range(HALF):
+                out_ref[b * BLK : (b + 1) * BLK, :] = acc_ref[b].astype(BF16)
+            masses_put(out_ref, mass_ref[...])
 
 
 def weighted_sums(by_src, picks, table, place, mine, other, mat, rows):
     width = rows.shape[2]
     return pl.pallas_call(
         functools.partial(sums_kernel, by_src),
-        out_shape=jax.ShapeDtypeStruct((len(picks), HALF_ROWS, width), BF16),
+        out_shape=(jax.ShapeDtypeStruct((HALF_ROWS, width), BF16),) * len(picks),
         grid=(len(picks),),
         in_specs=smem(3) + spec(4),
-        out_specs=pl.BlockSpec((1, HALF_ROWS, width), lambda q: (q, 0, 0)),
+        out_specs=tuple(spec(len(picks))),
         scratch_shapes=[pltpu.VMEM((HALF, BLK, width), F32), pltpu.VMEM((8, BLK), F32)],
-        compiler_params=pltpu.CompilerParams(vmem_limit_bytes=24 << 20),
+        compiler_params=pltpu.CompilerParams(vmem_limit_bytes=16 << 20),
         name="weighted_sums",
     )(table, place, jnp.array(picks, jnp.int32), mine, other, mat, rows)
 
 
-def add_kernel(a_ref, b_ref, out_ref):
+def add_kernel(which, a_ref, b_ref, *refs):
+    out_ref = refs[-1]
+    tail = slice(HALF * BLK, HALF_ROWS)
+    mass = masses_of(a_ref[tail, :])[0:OWN, :]
+    if which is not None:
+        mass = mass * refs[0][which]
     for b in range(HALF):
         rows = slice(b * BLK, (b + 1) * BLK)
-        out_ref[0, rows, :] = (a_ref[0, rows, :].astype(F32) + b_ref[0, rows, :].astype(F32)).astype(BF16)
-    tail = slice(HALF * BLK, HALF_ROWS)
-    mass = masses_of(a_ref[0, tail, :]) + masses_of(b_ref[0, tail, :])
-    masses_put(out_ref, 0, mass[0:8, :], out_ref.shape[2])
-
-
-def added(a, b):
-    return pl.pallas_call(
-        add_kernel,
+        total = a_ref[rows, :].astype(F32)
+        if which is not None:
+            total = total * jnp.broadcast_to(refs[0][which, b : b + 1, :], (BLK, BLK)).T[:, 0:1]
+        out_ref[rows, :] = (total + b_ref[rows, :].astype(F32)).astype(BF16)
+    masses_put(out_ref, mass + masses_of(b_ref[tail, :])[0:OWN, :])
+
+
+def added(a, b, which, shares):
+    given = () if shares is None else (shares,)
+    return pl.pallas_call(
+        functools.partial(add_kernel, None if shares is None else which),
         out_shape=jax.ShapeDtypeStruct(a.shape, BF16),
-        in_specs=spec(2),
+        in_specs=spec(2 + len(given)),
         out_specs=spec(1)[0],
         compiler_params=pltpu.CompilerParams(vmem_limit_bytes=8 << 20),
         name="added",
-    )(a, b)
+    )(a, b, *given)
 
 
 def mean_kernel(*refs):
@@ -450,11 +482,11 @@
     step = pl.program_id(0)
 
     def give(rows, tails, b):
-        mass = masses_of(tails[0][0])
-        total = rows[0][0].astype(F32)
+        mass = masses_of(tails[0])
+        total = rows[0][...].astype(F32)
         for row, tail in zip(rows[1:], tails[1:]):
-            mass = mass + masses_of(tail[0])
-            total = total + row[0].astype(F32)
+            mass = mass + masses_of(tail)
+            total = total + row[...].astype(F32)
         pick = lax.broadcasted_iota(jnp.int32, mass.shape, 0) == b
         line = jnp.sum(jnp.where(pick, mass, 0.0), axis=0, keepdims=True)
         share = jnp.broadcast_to(1.0 / line, (BLK, BLK)).T
@@ -470,13 +502,11 @@
 
 
 def mean_of(low, high):
-    width = low[0][0].shape[2]
-    loads, rows, tails = [], [], []
-    for group, at in ((low, lambda b: jnp.minimum(b, HALF - 1)), (high, lambda b: jnp.maximum(b - HALF, 0))):
-        for array, row in group:
-            loads.append(array)
-            rows.append(pl.BlockSpec((1, BLK, width), lambda b, row=row, at=at: (row, at(b), 0)))
-            tails.append(pl.BlockSpec((1, 16, width), lambda b, row=row: (row, HALF * BLK // 16, 0)))
+    width = low[0].shape[1]
+    loads, rows, tails = [*low, *high], [], []
+    for at in (lambda b: jnp.minimum(b, HALF - 1), lambda b: jnp.maximum(b - HALF, 0)):
+        rows += [pl.BlockSpec((BLK, width), lambda b, at=at: (at(b), 0))] * 3
+        tails += [pl.BlockSpec((16, width), lambda b: (HALF * BLK // 16, 0))] * 3
     return pl.pallas_call(
         mean_kernel,
         out_shape=jax.ShapeDtypeStruct((OWN * BLK, width), BF16),
@@ -505,17 +535,16 @@
 
 
 def far_sent(far, axis):
-    return shifted(far[0:1], axis, 1), shifted(far[1:2], axis, -1)
-
-
-def near_sent(near, far_low, far_high, axis):
-    plain_high = shifted(near[2:3], axis, 1)
-    plain_low = shifted(near[3:4], axis, -1)
-    sum_low = shifted(added(far_low, near[0:1]), axis, 1)
-    sum_high = shifted(added(far_high, near[1:2]), axis, -1)
-    low = [(near, 4), (plain_low, 0), (sum_low, 0)]
-    high = [(near, 5), (plain_high, 0), (sum_high, 0)]
-    return low, high
+    return shifted(far[0], axis, 1), shifted(far[1], axis, -1)
+
+
+def plain_sent(plain, axis):
+    return shifted(plain[0], axis, -1), shifted(plain[1], axis, 1)
+
+
+def joint_sent(joint, far, axis, shares=None):
+    low = shifted(added(far[0], joint[0], 0, shares), axis, 1)
+    return low, shifted(added(far[1], joint[1], 1, shares), axis, -1)
 
 
 def beside_core(value):
@@ -525,6 +554,17 @@
 def along_z(value, away):
     ring = [(k, (k // 2 + away) % SIDE * 2 + k % 2) for k in range(2 * SIDE)]
     return lax.ppermute(value, "wide", ring)
+
+
+def unpacked(facts, place):
+    facts = facts.reshape(SIDE, SIDE, LINES, BLK)
+    of_column = lax.dynamic_index_in_dim(facts, place[1], axis=1, keepdims=False)
+    of_row = lax.dynamic_index_in_dim(facts, place[0], axis=0, keepdims=False)
+    lists = of_column[:, 0, : OWN * LIST].astype(jnp.int32).reshape(-1)
+    ids = of_row[:, 1 : 1 + OWN].astype(jnp.int32).reshape(GROUP, BLK)
+    src_sq = of_column[:, 1 + OWN : 1 + 2 * OWN].reshape(GROUP, BLK)
+    tgt_sq = of_row[:, 1 + 2 * OWN :].reshape(GROUP, BLK)
+    return entry_table(lists, place), ids, src_sq, tgt_sq
 
 
 def square_norms(rows):
@@ -549,10 +589,10 @@
     w = lax.axis_index("wide")
     place = jnp.stack([y, x, w // 2, w % 2]).astype(jnp.int32)
 
+    rows = copied(centroids_src, NARROW).reshape(-1, width)
     cols = centroids_tgt.T
     cols = jnp.stack([cols, beside_core(cols)])
     cols = [cols] + [along_z(cols, away) for away in range(1, SIDE)]
-    rows = copied(centroids_src, NARROW).reshape(-1, width)
 
     facts = jnp.concatenate(
         [
@@ -563,49 +603,69 @@
         ],
         axis=0,
     )
-    facts = copied(facts, NARROW).reshape(SIDE, SIDE, LINES, BLK)
-    of_column = lax.dynamic_index_in_dim(facts, x, axis=1, keepdims=False)
-    of_row = lax.dynamic_index_in_dim(facts, y, axis=0, keepdims=False)
-    lists = of_column[:, 0, : OWN * LIST].astype(jnp.int32).reshape(-1)
-    ids = of_row[:, 1 : 1 + OWN].astype(jnp.int32).reshape(GROUP, BLK)
-    src_sq = of_column[:, 1 + OWN : 1 + 2 * OWN].reshape(GROUP, BLK)
-    tgt_sq = of_row[:, 1 + 2 * OWN :].reshape(GROUP, BLK)
-    table = entry_table(lists, place)
-
-    rows, sources, targets = lax.optimization_barrier((rows, sources, targets))
+    rows, cols, facts, sources, targets = lax.optimization_barrier(
+        (rows, cols, facts, sources, targets)
+    )
     all_targets = lax.all_gather(targets, "x", axis=0).reshape(GROUP, BLK, width)
     all_sources = lax.all_gather(sources, "y", axis=0).reshape(GROUP, BLK, width)
 
     by_col, by_row = coarse_costs(place, rows, cols, scale)
     row_mass = sender_mean_measure.reshape(-1, BLK)
     col_mass = recipient_mean_measure.reshape(-1, BLK)
-    recv = jnp.zeros((wide, *col_mass.shape), F32)
+    recv = facts
     for turn in range(ITC):
         sent = coarse_half(turn == 0, recv, col_mass, by_row, narrow)
-        sent = coarse_half(False, exchanged(sent, NARROW), row_mass, by_col, wide)
-        recv = exchanged(sent, "wide")
-        if turn == ITC - 3:
-            recv, table = lax.optimization_barrier((recv, table))
-        if turn == ITC - 2:
-            a, at = fine_costs(table, all_sources, all_targets, src_sq, tgt_sq, scale)
-            recv, a, at = lax.optimization_barrier((recv, a, at))
-    coarse = exchanged(coarse_end(recv, col_mass, narrow), NARROW).reshape(-1, BLK)
+        got = exchanged(sent, NARROW)
+        sent = coarse_half(False, got, row_mass, by_col, wide)
+        if turn == 0:
+            sent, got = lax.optimization_barrier((sent, got))
+            table, ids, src_sq, tgt_sq = unpacked(got[:, OWN:], place)
+            recv = exchanged(sent, "wide")
+            recv, table, ids, src_sq, tgt_sq = lax.optimization_barrier((recv, table, ids, src_sq, tgt_sq))
+        else:
+            recv = exchanged(sent, "wide")
+    sent = coarse_end(recv, col_mass, narrow)
+    sent, table = lax.optimization_barrier((sent, table))
+    a, at = fine_costs(table, all_sources, all_targets, src_sq, tgt_sq, scale)
+    coarse = exchanged(sent, NARROW).reshape(-1, BLK)
 
     given, first = (coarse, ids), True
     for step in range(STEPS):
-        src_parts = exchanged(fine_half(first, AT_TGT, AT_SRC, table, given, at), "y")
-        tgt_parts = exchanged(fine_half(False, AT_SRC, AT_TGT, table, (src_parts,), a), "x")
+        last = step == STEPS - 1
+        sent = fine_half(first, False, AT_TGT, AT_SRC, table, given, at)
+        src_parts = exchanged(sent, "y")
+        sent = fine_half(False, last, AT_SRC, AT_TGT, table, (src_parts,), a)
+        sent, s_pot = sent if last else (sent, None)
+        tgt_parts = exchanged(sent, "x")
         given, first = (tgt_parts,), False
 
-    s_pot, t_pot, s_own, t_own = final_potentials(place, src_parts, tgt_parts)
-    src_args = (table, place, s_pot, t_pot, a, all_targets)
-    tgt_args = (table, place, t_pot, s_pot, at, all_sources)
-    src_far = far_sent(weighted_sums(True, FAR, *src_args), "y")
-    tgt_far = far_sent(weighted_sums(False, FAR, *tgt_args), "x")
-    src_near = weighted_sums(True, NEAR, *src_args)
-    tgt_near = weighted_sums(False, NEAR, *tgt_args)
-    src_mean = mean_of(*near_sent(src_near, *src_far, "y"))
-    tgt_mean = mean_of(*near_sent(tgt_near, *tgt_far, "x"))
+    def src_sums(picks, t_pot):
+        return weighted_sums(True, picks, table, place, s_pot, t_pot, a, all_targets)
+
+    def tgt_sums(picks, mine):
+        return weighted_sums(False, picks, table, place, mine, s_pot, at, all_sources)
+
+    tgt_far = tgt_sums(FAR, sent)
+    tgt_far = far_sent(tgt_far, "x")
+    t_pot, s_own, t_own, shares = final_potentials(place, s_pot, tgt_parts)
+    src_far = src_sums(FAR, t_pot)
+    src_far, t_pot = lax.optimization_barrier((src_far, t_pot))
+    src_far = far_sent(src_far, "y")
+    tgt_plain = tgt_sums(PLAIN, t_pot)
+    tgt_plain, t_pot = lax.optimization_barrier((tgt_plain, t_pot))
+    tgt_plain = plain_sent(tgt_plain, "x")
+    src_near = src_sums(PLAIN + JOINT, t_pot)
+    src_near, t_pot = lax.optimization_barrier((src_near, t_pot))
+    src_plain = plain_sent(src_near[0:2], "y")
+    tgt_near = tgt_sums(JOINT + HOME, t_pot)
+    tgt_near, tgt_far = lax.optimization_barrier((tgt_near, tgt_far))
+    tgt_joint = joint_sent(tgt_near[0:2], tgt_far, "x", shares)
+    src_joint = joint_sent(src_near[2:4], src_far, "y")
+    late = t_pot
+    src_home = src_sums(HOME, late)
+    tgt_home = tgt_near[2:4]
+    tgt_mean = mean_of(*([tgt_home[k], tgt_plain[k], tgt_joint[k]] for k in range(2)))
+    src_mean = mean_of(*([src_home[k], src_plain[k], src_joint[k]] for k in range(2)))
     return src_mean, tgt_mean, s_own.reshape(-1), t_own.reshape(-1)
 
 

time: 387 us -> 359 us (0.928)
  blocking collectives: 99.1 us -> 154 us
  waiting for transfers between devices: 111 us -> 56.1 us
  starting transfers between devices: 58.8 us -> 43.1 us
  Pallas kernels: 80.5 us -> 69.9 us
    all_to_all x9 -> x16, blocking collectives: 99.1 us -> 154 us  [exchanged(): return lax.all_to_all(copies, axis, split_axis=0, concat_axis=0, tiled=True)]
    all_to_all x12 -> x4, waiting for transfers between devices: 64.7 us -> 17.3 us  [exchanged(): return lax.all_to_all(copies, axis, split_axis=0, concat_axis=0, tiled=True)]
    all_to_all x12 -> x4, starting transfers between devices: 42.8 us -> 19.5 us  [exchanged(): return lax.all_to_all(copies, axis, split_axis=0, concat_axis=0, tiled=True)]
    pallas_call x1, Pallas kernels: 11.6 us -> 4.86 us  [fine_costs(): pl.pallas_call(functools.partial(fine_cost_kernel, scale), out_shape=(sha...]
    ppermute x12, starting transfers between devices: 10.6 us -> 16.9 us  [shifted(): lax.ppermute(value, axis, [(k, (k + away) % SIDE) for k in range(SIDE)])]
    pallas_call x12, Pallas kernels: 19 us -> 13.3 us  [coarse_half(): pl.pallas_call(functools.partial(coarse_half_kernel, first), out_shape=ja...]
    ppermute x3, waiting for transfers between devices: 10.8 us -> 6.16 us  [along_z(): return lax.ppermute(value, 'wide', ring)]
    pallas_call x15 -> x17, Pallas kernels: 33 us -> 34.8 us  [the longest x6 18 us: weighted_sums(): pl.pallas_call(functools.partial(sums_kernel, by_src), out_shape=(jax.Sha...]
  transfers between devices with their start and end apart: 30 -> 22, of which waited for: 21 -> 11; matrix products, arithmetic and copies ran while one was open for 2% -> 1% of each run, Pallas kernels for 14% -> 14%
where the time goes in v2:
time: 359 us; the launch traced here: 357 us
  blocking collectives  154 us (43%)
  Pallas kernels  69.9 us (19%)
  waiting for transfers between devices  56.1 us (16%)
  starting transfers between devices  43.1 us (12%)
  local copies, waits for them, and re-layouts  17.1 us (5%)
  between operations  14.6 us (4%)
    all_to_all x16, blocking collectives, exchanged(): return lax.all_to_all(copies, axis, split_axis=0, concat_axis=0, tiled=True)  154 us
    ppermute x12, waiting for transfers between devices, shifted(): lax.ppermute(value, axis, [(k, (k + away) % SIDE) for k in range(SIDE)])  31 us
    all_to_all x4, starting transfers between devices, exchanged(): return lax.all_to_all(copies, axis, split_axis=0, concat_axis=0, tiled=True)  19.5 us
    pallas_call x6, Pallas kernels, weighted_sums(): pl.pallas_call(functools.partial(sums_kernel, by_src), out_shape=(jax.Sha...  18 us
    all_to_all x4, waiting for transfers between devices, exchanged(): return lax.all_to_all(copies, axis, split_axis=0, concat_axis=0, tiled=True)  17.3 us
    ppermute x12, starting transfers between devices, shifted(): lax.ppermute(value, axis, [(k, (k + away) % SIDE) for k in range(SIDE)])  16.9 us
    pallas_call x6, Pallas kernels, fine_half(): pl.pallas_call(functools.partial(fine_half_kernel, first, last, given_at,...  14.5 us
    unnamed x50, local copies, waits for them, and re-layouts  13.9 us
  transfers between devices with their start and end apart: 22, of which 11 were waited for; matrix products, arithmetic and copies ran while one was open for 1% of the time, Pallas kernels for 14%

profile of v2, /device:TPU:0, one launch (start us, length us, event | category | flops | bytes accessed | tf_op | source)
XLA Modules:
  0.0 357.5 jit_solution(8556071876652821581)
XLA Ops:
  9.5 7.1 %all-to-all-start = ((bf16[16,64,768]{2,1,0:T(8,128)(2,1)}), bf16[16,64,768]{2,1,0:T(8,128)(2,1)S(1)}, u32[]{:S(2)}, u32[]{:S(2)}) async-start(bf16[16,64,768]{2,1,0:T(8,128)(2,1)} %broadcast_in_dim.3), calls=%async_computation | async-start | bytes 3145728 | tf_op jit(solution)/shard_map/all_to_all | solution.py:525
  27.5 5.4 %collective-permute-done.2.refs_2_ = bf16[2,96,512]{2,1,0:T(8,128)(2,1)S(1)} collective-permute-done((bf16[2,96,512]{2,1,0:T(8,128)(2,1)S(1)}, bf16[2,96,512]{2,1,0:T(8,128)(2,1)S(1)}, u32[]{:S(2)}, u32[]{:S(2)}) %collective-permute-start.2) | collective-permute-done | bytes 196640 | tf_op jit(solution)/shard_map/ppermute | solution.py:556
  32.9 8.3 %all-to-all-done = bf16[16,64,768]{2,1,0:T(8,128)(2,1)S(1)} async-done(((bf16[16,64,768]{2,1,0:T(8,128)(2,1)}), bf16[16,64,768]{2,1,0:T(8,128)(2,1)S(1)}, u32[]{:S(2)}, u32[]{:S(2)}) %all-to-all-start) | async-done | bytes 1572896 | tf_op jit(solution)/shard_map/all_to_all | solution.py:525
  53.8 9.0 %all-to-all-done.1.recv_ref = f32[16,33,128]{2,1,0:T(8,128)S(1)} async-done(((f32[16,33,128]{2,1,0:T(8,128)}), f32[16,33,128]{2,1,0:T(8,128)S(1)}, u32[]{:S(2)}, u32[]{:S(2)}) %all-to-all-start.1) | async-done | bytes 270368 | tf_op jit(solution)/shard_map/all_to_all | solution.py:525
  64.4 5.3 %all-to-all-start.2 = ((f32[8,4,128]{2,1,0:T(4,128)}), f32[8,4,128]{2,1,0:T(4,128)S(1)}, u32[]{:S(2)}, u32[]{:S(2)}) async-start(f32[8,4,128]{2,1,0:T(4,128)} %coarse_half.13), calls=%async_computation.2 | async-start | bytes 32768 | tf_op jit(solution)/shard_map/all_to_all | solution.py:525
  70.5 4.6 %entry_table.1.table_ref.refs_0_ = s32[768]{0:T(1024)} custom-call(s32[128]{0:T(128)} %convert_element_type.45.lists_ref, s32[4]{0:T(128)} %copy-done.13), custom_call_target="tpu_custom_call" | custom-call | tf_op jit(solution)/shard_map/entry_table/pallas_call | solution.py:212
  77.8 11.5 %all_to_all.100.recv_ref = f32[16,8,128]{2,1,0:T(8,128)S(1)} all-to-all(f32[16,8,128]{2,1,0:T(8,128)S(1)} %coarse_half.14), channel_id=1, replica_groups=mesh['wide'=8,'y'=4,'x'=4] {'y','x'}, dimensions={0} | all-to-all | bytes 131072 | tf_op jit(solution)/shard_map/all_to_all | solution.py:525
  90.2 10.0 %all_to_all.101.recv_ref = f32[8,4,128]{2,1,0:T(4,128)S(1)} all-to-all(f32[8,4,128]{2,1,0:T(4,128)S(1)} %coarse_half.15), channel_id=1, replica_groups=mesh['wide'=8,'y'=4,'x'=4] {'wide'}, dimensions={0} | all-to-all | bytes 32768 | tf_op jit(solution)/shard_map/all_to_all | solution.py:525
  101.2 10.9 %all_to_all.102.recv_ref = f32[16,8,128]{2,1,0:T(8,128)S(1)} all-to-all(f32[16,8,128]{2,1,0:T(8,128)S(1)} %coarse_half.16), channel_id=1, replica_groups=mesh['wide'=8,'y'=4,'x'=4] {'y','x'}, dimensions={0} | all-to-all | bytes 131072 | tf_op jit(solution)/shard_map/all_to_all | solution.py:525
  113.1 7.7 %all_to_all.103.recv_ref = f32[8,4,128]{2,1,0:T(4,128)S(1)} all-to-all(f32[8,4,128]{2,1,0:T(4,128)S(1)} %coarse_half.17), channel_id=1, replica_groups=mesh['wide'=8,'y'=4,'x'=4] {'wide'}, dimensions={0} | all-to-all | bytes 32768 | tf_op jit(solution)/shard_map/all_to_all | solution.py:525
  121.9 11.7 %all_to_all.104.recv_ref = f32[16,8,128]{2,1,0:T(8,128)S(1)} all-to-all(f32[16,8,128]{2,1,0:T(8,128)S(1)} %coarse_half.18), channel_id=1, replica_groups=mesh['wide'=8,'y'=4,'x'=4] {'y','x'}, dimensions={0} | all-to-all | bytes 131072 | tf_op jit(solution)/shard_map/all_to_all | solution.py:525
  134.6 7.7 %all_to_all.105.recv_ref = f32[8,4,128]{2,1,0:T(4,128)S(1)} all-to-all(f32[8,4,128]{2,1,0:T(4,128)S(1)} %coarse_half.19), channel_id=1, replica_groups=mesh['wide'=8,'y'=4,'x'=4] {'wide'}, dimensions={0} | all-to-all | bytes 32768 | tf_op jit(solution)/shard_map/all_to_all | solution.py:525
  143.3 11.4 %all_to_all.106.recv_ref = f32[16,8,128]{2,1,0:T(8,128)S(1)} all-to-all(f32[16,8,128]{2,1,0:T(8,128)S(1)} %coarse_half.20), channel_id=1, replica_groups=mesh['wide'=8,'y'=4,'x'=4] {'y','x'}, dimensions={0} | all-to-all | bytes 131072 | tf_op jit(solution)/shard_map/all_to_all | solution.py:525
  155.7 7.7 %all_to_all.107.recv_ref = f32[8,4,128]{2,1,0:T(4,128)S(1)} all-to-all(f32[8,4,128]{2,1,0:T(4,128)S(1)} %coarse_half.21), channel_id=1, replica_groups=mesh['wide'=8,'y'=4,'x'=4] {'wide'}, dimensions={0} | all-to-all | bytes 32768 | tf_op jit(solution)/shard_map/all_to_all | solution.py:525
  164.5 11.4 %all_to_all.108.recv_ref = f32[16,8,128]{2,1,0:T(8,128)S(1)} all-to-all(f32[16,8,128]{2,1,0:T(8,128)S(1)} %coarse_half.22), channel_id=1, replica_groups=mesh['wide'=8,'y'=4,'x'=4] {'y','x'}, dimensions={0} | all-to-all | bytes 131072 | tf_op jit(solution)/shard_map/all_to_all | solution.py:525
  176.9 8.2 %all_to_all.109.recv_ref = f32[8,4,128]{2,1,0:T(4,128)} all-to-all(f32[8,4,128]{2,1,0:T(4,128)S(1)} %coarse_half.23), channel_id=1, replica_groups=mesh['wide'=8,'y'=4,'x'=4] {'wide'}, dimensions={0} | all-to-all | bytes 32768 | tf_op jit(solution)/shard_map/all_to_all | solution.py:525
  195.6 4.9 %fine_costs.1 = (f32[52,128,128]{2,1,0:T(8,128)S(1)}, f32[52,128,128]{2,1,0:T(8,128)S(1)}) custom-call(s32[768]{0:T(1024)S(1)} %copy-done.10, bf16[32,128,768]{2,1,0:T(8,128)(2,1)S(1)} %bitcast.40, bf16[32,128,768]{2,1,0:T(8,128)(2,1)S(1)} %bitcast.34, f32[32,128]{1,0:T(8,128)S(1)} %get-tuple-element.81.xsq_ref, f32[32,128]{1,0:T(8,128)S(1)} %get-tuple-element.82.ysq_ref), custom_call_target="tpu_custom_call" | custom-call | tf_op jit(solution)/shard_map/fine_costs/pallas_call | solution.py:242
  204.2 4.1 %fine_half.6 = f32[4,32,128]{2,1,0:T(8,128)S(1)} custom-call(s32[768]{0:T(1024)S(1)} %copy-done.10, f32[64,128]{1,0:T(8,128)S(1)} %bitcast.51, s32[32,128]{1,0:T(8,128)S(1)} %get-tuple-element.78.refs_2_, f32[52,128,128]{2,1,0:T(8,128)S(1)} %copy-done.1), custom_call_target="tpu_custom_call" | custom-call | tf_op jit(solution)/shard_map/fine_half/pallas_call | solution.py:326
  208.3 10.3 %all_to_all.110.refs_1_ = f32[4,32,128]{2,1,0:T(8,128)S(1)} all-to-all(f32[4,32,128]{2,1,0:T(8,128)S(1)} %fine_half.6), channel_id=1, replica_groups=mesh['wide'=8,'y'=4,'x'=4] {'y'}, dimensions={0} | all-to-all | bytes 131072 | tf_op jit(solution)/shard_map/all_to_all | solution.py:525
  220.6 9.9 %all_to_all.111.refs_1_ = f32[4,32,128]{2,1,0:T(8,128)S(1)} all-to-all(f32[4,32,128]{2,1,0:T(8,128)S(1)} %fine_half.7), channel_id=1, replica_groups=mesh['wide'=8,'y'=4,'x'=4] {'x'}, dimensions={0} | all-to-all | bytes 131072 | tf_op jit(solution)/shard_map/all_to_all | solution.py:525
  232.7 8.0 %all_to_all.112.refs_1_ = f32[4,32,128]{2,1,0:T(8,128)S(1)} all-to-all(f32[4,32,128]{2,1,0:T(8,128)S(1)} %fine_half.8), channel_id=1, replica_groups=mesh['wide'=8,'y'=4,'x'=4] {'y'}, dimensions={0} | all-to-all | bytes 131072 | tf_op jit(solution)/shard_map/all_to_all | solution.py:525
  242.8 8.0 %all_to_all.113.refs_1_ = f32[4,32,128]{2,1,0:T(8,128)S(1)} all-to-all(f32[4,32,128]{2,1,0:T(8,128)S(1)} %fine_half.9), channel_id=1, replica_groups=mesh['wide'=8,'y'=4,'x'=4] {'x'}, dimensions={0} | all-to-all | bytes 131072 | tf_op jit(solution)/shard_map/all_to_all | solution.py:525
  252.9 8.3 %all_to_all.114.refs_1_ = f32[4,32,128]{2,1,0:T(8,128)S(1)} all-to-all(f32[4,32,128]{2,1,0:T(8,128)S(1)} %fine_half.10), channel_id=1, replica_groups=mesh['wide'=8,'y'=4,'x'=4] {'y'}, dimensions={0} | all-to-all | bytes 131072 | tf_op jit(solution)/shard_map/all_to_all | solution.py:525
  269.5 11.5 %all_to_all.115.trecv_ref = f32[4,32,128]{2,1,0:T(8,128)S(1)} all-to-all(f32[4,32,128]{2,1,0:T(8,128)S(1)} %get-tuple-element.86.mine_ref), channel_id=1, replica_groups=mesh['wide'=8,'y'=4,'x'=4] {'x'}, dimensions={0} | all-to-all | bytes 131072 | tf_op jit(solution)/shard_map/all_to_all | solution.py:525
  287.1 3.8 %weighted_sums.8 = (bf16[528,768]{1,0:T(8,128)(2,1)S(1)}, bf16[528,768]{1,0:T(8,128)(2,1)S(1)}, bf16[528,768]{1,0:T(8,128)(2,1)S(1)}, bf16[528,768]{1,0:T(8,128)(2,1)S(1)}) custom-call(s32[768]{0:T(1024)S(1)} %copy-done.10, s32[4]{0:T(128)S(1)} %copy-done.14, s32[4]{0:T(128)S(1)} %copy-done.17, f32[32,128]{1,0:T(8,128)S(1)} %get-tuple-element.85.s_ref.mine_ref.other_ref, ...), custom_call_target="tpu_custom_call" | custom-call | tf_op jit(solution)/shard_map/weighted_sums/pallas_call | solution.py:441
  294.3 3.8 %collective-permute-start.12 = (bf16[528,768]{1,0:T(8,128)(2,1)S(1)}, bf16[528,768]{1,0:T(8,128)(2,1)S(1)}, u32[]{:S(2)}, u32[]{:S(2)}) collective-permute-start(bf16[528,768]{1,0:T(8,128)(2,1)S(1)} %get-tuple-element.114), channel_id=1, source_target_pairs={{0,3},{1,0},{2,1},{3,2},{4,7},{5,4},{6,5},{7,6},{8,11},{9,8},{10,9... | collective-permute-start | bytes 2433032 | tf_op jit(solution)/shard_map/ppermute | solution.py:534
  298.1 4.1 %weighted_sums.10 = (bf16[528,768]{1,0:T(8,128)(2,1)S(1)}, bf16[528,768]{1,0:T(8,128)(2,1)S(1)}, bf16[528,768]{1,0:T(8,128)(2,1)S(1)}, bf16[528,768]{1,0:T(8,128)(2,1)S(1)}) custom-call(s32[768]{0:T(1024)S(1)} %copy-done.10, s32[4]{0:T(128)S(1)} %copy-done.14, s32[4]{0:T(128)S(1)} %copy-done.16, f32[32,128]{1,0:T(8,128)S(1)} %get-tuple-element.98.other_ref.mine_ref, ...), custom_call_target="tpu_custom_call" | custom-call | tf_op jit(solution)/shard_map/weighted_sums/pallas_call | solution.py:441
  305.8 5.2 %collective-permute-done.8.a_ref = bf16[528,768]{1,0:T(8,128)(2,1)S(1)} collective-permute-done((bf16[528,768]{1,0:T(8,128)(2,1)S(1)}, bf16[528,768]{1,0:T(8,128)(2,1)S(1)}, u32[]{:S(2)}, u32[]{:S(2)}) %collective-permute-start.8) | collective-permute-done | bytes 811040 | tf_op jit(solution)/shard_map/ppermute | solution.py:534
  311.0 4.0 %collective-permute-start.15 = (bf16[528,768]{1,0:T(8,128)(2,1)S(1)}, bf16[528,768]{1,0:T(8,128)(2,1)S(1)}, u32[]{:S(2)}, u32[]{:S(2)}) collective-permute-start(bf16[528,768]{1,0:T(8,128)(2,1)S(1)} %added.7), channel_id=1, source_target_pairs={{0,3},{1,0},{2,1},{3,2},{4,7},{5,4},{6,5},{7,6},{8,11},{9,8},{10,9... | collective-permute-start | bytes 2433032 | tf_op jit(solution)/shard_map/ppermute | solution.py:534
  316.2 8.2 %collective-permute-done.14.refs_4_.refs_10_ = bf16[528,768]{1,0:T(8,128)(2,1)S(1)} collective-permute-done((bf16[528,768]{1,0:T(8,128)(2,1)S(1)}, bf16[528,768]{1,0:T(8,128)(2,1)S(1)}, u32[]{:S(2)}, u32[]{:S(2)}) %collective-permute-start.14) | collective-permute-done | bytes 811040 | tf_op jit(solution)/shard_map/ppermute | solution.py:534
  324.5 9.8 %collective-permute-done.13.refs_2_.refs_8_ = bf16[528,768]{1,0:T(8,128)(2,1)S(1)} collective-permute-done((bf16[528,768]{1,0:T(8,128)(2,1)S(1)}, bf16[528,768]{1,0:T(8,128)(2,1)S(1)}, u32[]{:S(2)}, u32[]{:S(2)}) %collective-permute-start.13) | collective-permute-done | bytes 811040 | tf_op jit(solution)/shard_map/ppermute | solution.py:534
  340.4 6.5 %collective-permute-done.9.refs_5_.refs_11_ = bf16[528,768]{1,0:T(8,128)(2,1)S(1)} collective-permute-done((bf16[528,768]{1,0:T(8,128)(2,1)S(1)}, bf16[528,768]{1,0:T(8,128)(2,1)S(1)}, u32[]{:S(2)}, u32[]{:S(2)}) %collective-permute-start.9) | collective-permute-done | bytes 811040 | tf_op jit(solution)/shard_map/ppermute | solution.py:534
  (135 shorter events, 94.4 us)
Async XLA Ops:
  9.5 31.7 %all-to-all-start = ((bf16[16,64,768]{2,1,0:T(8,128)(2,1)}), bf16[16,64,768]{2,1,0:T(8,128)(2,1)S(1)}, u32[]{:S(2)}, u32[]{:S(2)}) async-start(bf16[16,64,768]{2,1,0:T(8,128)(2,1)} %broadcast_in_dim.3), calls=%async_computation | async-start | bytes 3145728 | tf_op jit(solution)/shard_map/all_to_all | solution.py:525
  16.7 9.8 %copy-start.22 = (s32[8,4]{0,1:T(4,128)S(1)}, s32[8,4]{0,1:T(4,128)}, u32[]{:S(2)}) copy-start(s32[8,4]{0,1:T(4,128)} %param.16) | copy-start | bytes 388
  16.7 173.3 %all-gather.5.cloned.1.call-start = ((), (), s32[]{:S(2)}) async-start(), calls=%async_computation.20 | async-start | bytes 7864320 | tf_op jit(solution)/shard_map/all_gather | solution.py:610
  16.7 1.4 collective-permute-start
  18.1 9.3 %collective-permute-start.1 = (bf16[2,96,512]{2,1,0:T(8,128)(2,1)S(1)}, bf16[2,96,512]{2,1,0:T(8,128)(2,1)S(1)}, u32[]{:S(2)}, u32[]{:S(2)}) collective-permute-start(bf16[2,96,512]{2,1,0:T(8,128)(2,1)S(1)} %pad_maximum_fusion.refs_0_), channel_id=1, source_target_pairs={{0,32},{16,48},{32,64},{48,80},{64,96},{80,112},{96,0},{112,16},{1... | collective-permute-start | bytes 589832 | tf_op jit(solution)/shard_map/ppermute | solution.py:556
  20.1 12.7 %collective-permute-start.2 = (bf16[2,96,512]{2,1,0:T(8,128)(2,1)S(1)}, bf16[2,96,512]{2,1,0:T(8,128)(2,1)S(1)}, u32[]{:S(2)}, u32[]{:S(2)}) collective-permute-start(bf16[2,96,512]{2,1,0:T(8,128)(2,1)S(1)} %pad_maximum_fusion.refs_0_), channel_id=1, source_target_pairs={{0,64},{16,80},{32,96},{48,112},{64,0},{80,16},{96,32},{112,48},{1... | collective-permute-start | bytes 589832 | tf_op jit(solution)/shard_map/ppermute | solution.py:556
  23.7 9.1 %collective-permute-start.3 = (bf16[2,96,512]{2,1,0:T(8,128)(2,1)S(1)}, bf16[2,96,512]{2,1,0:T(8,128)(2,1)S(1)}, u32[]{:S(2)}, u32[]{:S(2)}) collective-permute-start(bf16[2,96,512]{2,1,0:T(8,128)(2,1)S(1)} %pad_maximum_fusion.refs_0_), channel_id=1, source_target_pairs={{0,96},{16,112},{32,0},{48,16},{64,32},{80,48},{96,64},{112,80},{1... | collective-permute-start | bytes 589832 | tf_op jit(solution)/shard_map/ppermute | solution.py:556
  41.2 148.8 %all-gather.7.cloned.1.call-start = ((), (), s32[]{:S(2)}) async-start(), calls=%async_computation.21 | async-start | bytes 7864320 | tf_op jit(solution)/shard_map/all_gather | solution.py:609
  47.3 15.5 %copy-start.11 = (f32[1024]{0:T(1024)S(1)}, f32[1024]{0:T(1024)}, u32[]{:S(2)}) copy-start(f32[1024]{0:T(1024)} %param.20) | copy-start | bytes 12292
  50.2 12.6 %all-to-all-start.1 = ((f32[16,33,128]{2,1,0:T(8,128)}), f32[16,33,128]{2,1,0:T(8,128)S(1)}, u32[]{:S(2)}, u32[]{:S(2)}) async-start(f32[16,33,128]{2,1,0:T(8,128)} %coarse_half.12), calls=%async_computation.1 | async-start | bytes 655360 | tf_op jit(solution)/shard_map/all_to_all | solution.py:525
  64.4 10.7 %all-to-all-start.2 = ((f32[8,4,128]{2,1,0:T(4,128)}), f32[8,4,128]{2,1,0:T(4,128)S(1)}, u32[]{:S(2)}, u32[]{:S(2)}) async-start(f32[8,4,128]{2,1,0:T(4,128)} %coarse_half.13), calls=%async_computation.2 | async-start | bytes 32768 | tf_op jit(solution)/shard_map/all_to_all | solution.py:525
  163.4 26.6 %copy-start.10 = (s32[768]{0:T(1024)S(1)}, s32[768]{0:T(1024)}, u32[]{:S(2)}) copy-start(s32[768]{0:T(1024)} %entry_table.1.table_ref.refs_0_) | copy-start | bytes 9220
  186.5 15.7 %all-to-all-start.13 = ((f32[16,4,128]{2,1,0:T(4,128)}), f32[16,4,128]{2,1,0:T(4,128)S(1)}, u32[]{:S(2)}, u32[]{:S(2)}) async-start(f32[16,4,128]{2,1,0:T(4,128)} %coarse_end.1), calls=%async_computation.13 | async-start | bytes 65536 | tf_op jit(solution)/shard_map/all_to_all | solution.py:525
  230.6 51.6 %slice-start = ((s8[6291456]{0:T(1024)(128)(4,1)}), s8[4194304]{0:T(1024)(128)(4,1)S(1)}, s32[]{:S(2)}) async-start(s8[6291456]{0:T(1024)(128)(4,1)} %bitcast.35), calls=%async_computation.22 | async-start | bytes 8388608
  240.7 22.6 %copy-start.5 = (bf16[4096,768]{1,0:T(8,128)(2,1)S(1)}, bf16[4096,768]{1,0:T(8,128)(2,1)}, u32[]{:S(2)}) copy-start(bf16[4096,768]{1,0:T(8,128)(2,1)} %all-gather.5.cloned.1.call-done) | copy-start | bytes 18874372
  252.9 10.4 %copy-start.2 = (f32[52,128,128]{2,1,0:T(8,128)S(1)}, f32[52,128,128]{2,1,0:T(8,128)}, u32[]{:S(2)}) copy-start(f32[52,128,128]{2,1,0:T(8,128)} %copy-done) | copy-start | bytes 10223620
  252.9 10.4 %copy-start.14 = (s32[4]{0:T(128)S(1)}, s32[4]{0:T(128)}, u32[]{:S(2)}) copy-start(s32[4]{0:T(128)} %copy-done.13) | copy-start | bytes 52
  252.9 10.4 %copy-start.15 = (s32[2]{0:T(128)S(1)}, s32[2]{0:T(128)}, u32[]{:S(2)}) copy-start(s32[2]{0:T(128)} %constant.60.clone.picks_ref) | copy-start | bytes 28
  261.2 20.9 %slice-start.1 = ((s8[6291456]{0:T(1024)(128)(4,1)}), s8[2097152]{0:T(1024)(128)(4,1)S(1)}, s32[]{:S(2)}) async-start(s8[6291456]{0:T(1024)(128)(4,1)} %bitcast.35), calls=%async_computation.23 | async-start | bytes 4194304
  266.2 36.0 %collective-permute-start.10 = (bf16[528,768]{1,0:T(8,128)(2,1)S(1)}, bf16[528,768]{1,0:T(8,128)(2,1)S(1)}, u32[]{:S(2)}, u32[]{:S(2)}) collective-permute-start(bf16[528,768]{1,0:T(8,128)(2,1)S(1)} %get-tuple-element.111), channel_id=1, source_target_pairs={{0,1},{1,2},{2,3},{3,0},{4,5},{5,6},{6,7},{7,4},{8,9},{9,10},{10,1... | collective-permute-start | bytes 2433032 | tf_op jit(solution)/shard_map/ppermute | solution.py:534
  266.3 36.0 %collective-permute-start.11 = (bf16[528,768]{1,0:T(8,128)(2,1)S(1)}, bf16[528,768]{1,0:T(8,128)(2,1)S(1)}, u32[]{:S(2)}, u32[]{:S(2)}) collective-permute-start(bf16[528,768]{1,0:T(8,128)(2,1)S(1)} %get-tuple-element.112), channel_id=1, source_target_pairs={{0,3},{1,0},{2,1},{3,2},{4,7},{5,4},{6,5},{7,6},{8,11},{9,8},{10,9... | collective-permute-start | bytes 2433032 | tf_op jit(solution)/shard_map/ppermute | solution.py:534
  287.1 10.9 %copy-start.16 = (s32[4]{0:T(128)S(1)}, s32[4]{0:T(128)}, u32[]{:S(2)}) copy-start(s32[4]{0:T(128)} %constant.63.clone.picks_ref) | copy-start | bytes 52
  291.0 13.5 %collective-permute-start.5 = (bf16[528,768]{1,0:T(8,128)(2,1)S(1)}, bf16[528,768]{1,0:T(8,128)(2,1)S(1)}, u32[]{:S(2)}, u32[]{:S(2)}) collective-permute-start(bf16[528,768]{1,0:T(8,128)(2,1)S(1)} %get-tuple-element.101), channel_id=1, source_target_pairs={{0,4},{4,8},{8,12},{12,0},{1,5},{5,9},{9,13},{13,1},{2,6},{6,10},{... | collective-permute-start | bytes 2433032 | tf_op jit(solution)/shard_map/ppermute | solution.py:534
  292.7 18.2 %collective-permute-start.8 = (bf16[528,768]{1,0:T(8,128)(2,1)S(1)}, bf16[528,768]{1,0:T(8,128)(2,1)S(1)}, u32[]{:S(2)}, u32[]{:S(2)}) collective-permute-start(bf16[528,768]{1,0:T(8,128)(2,1)S(1)} %get-tuple-element.105), channel_id=1, source_target_pairs={{0,12},{4,0},{8,4},{12,8},{1,13},{5,1},{9,5},{13,9},{2,14},{6,2},{... | collective-permute-start | bytes 2433032 | tf_op jit(solution)/shard_map/ppermute | solution.py:534
  294.3 20.9 %collective-permute-start.12 = (bf16[528,768]{1,0:T(8,128)(2,1)S(1)}, bf16[528,768]{1,0:T(8,128)(2,1)S(1)}, u32[]{:S(2)}, u32[]{:S(2)}) collective-permute-start(bf16[528,768]{1,0:T(8,128)(2,1)S(1)} %get-tuple-element.114), channel_id=1, source_target_pairs={{0,3},{1,0},{2,1},{3,2},{4,7},{5,4},{6,5},{7,6},{8,11},{9,8},{10,9... | collective-permute-start | bytes 2433032 | tf_op jit(solution)/shard_map/ppermute | solution.py:534
  302.2 22.2 %collective-permute-start.14 = (bf16[528,768]{1,0:T(8,128)(2,1)S(1)}, bf16[528,768]{1,0:T(8,128)(2,1)S(1)}, u32[]{:S(2)}, u32[]{:S(2)}) collective-permute-start(bf16[528,768]{1,0:T(8,128)(2,1)S(1)} %get-tuple-element.119), channel_id=1, source_target_pairs={{0,1},{1,2},{2,3},{3,0},{4,5},{5,6},{6,7},{7,4},{8,9},{9,10},{10,1... | collective-permute-start | bytes 2433032 | tf_op jit(solution)/shard_map/ppermute | solution.py:534
  302.7 31.6 %collective-permute-start.13 = (bf16[528,768]{1,0:T(8,128)(2,1)S(1)}, bf16[528,768]{1,0:T(8,128)(2,1)S(1)}, u32[]{:S(2)}, u32[]{:S(2)}) collective-permute-start(bf16[528,768]{1,0:T(8,128)(2,1)S(1)} %added.6), channel_id=1, source_target_pairs={{0,1},{1,2},{2,3},{3,0},{4,5},{5,6},{6,7},{7,4},{8,9},{9,10},{10,1... | collective-permute-start | bytes 2433032 | tf_op jit(solution)/shard_map/ppermute | solution.py:534
  304.5 35.8 %collective-permute-start.4 = (bf16[528,768]{1,0:T(8,128)(2,1)S(1)}, bf16[528,768]{1,0:T(8,128)(2,1)S(1)}, u32[]{:S(2)}, u32[]{:S(2)}) collective-permute-start(bf16[528,768]{1,0:T(8,128)(2,1)S(1)} %get-tuple-element.100), channel_id=1, source_target_pairs={{0,12},{4,0},{8,4},{12,8},{1,13},{5,1},{9,5},{13,9},{2,14},{6,2},{... | collective-permute-start | bytes 2433032 | tf_op jit(solution)/shard_map/ppermute | solution.py:534
  311.0 25.6 %collective-permute-start.15 = (bf16[528,768]{1,0:T(8,128)(2,1)S(1)}, bf16[528,768]{1,0:T(8,128)(2,1)S(1)}, u32[]{:S(2)}, u32[]{:S(2)}) collective-permute-start(bf16[528,768]{1,0:T(8,128)(2,1)S(1)} %added.7), channel_id=1, source_target_pairs={{0,3},{1,0},{2,1},{3,2},{4,7},{5,4},{6,5},{7,6},{8,11},{9,8},{10,9... | collective-permute-start | bytes 2433032 | tf_op jit(solution)/shard_map/ppermute | solution.py:534
  315.2 25.2 %collective-permute-start.7 = (bf16[528,768]{1,0:T(8,128)(2,1)S(1)}, bf16[528,768]{1,0:T(8,128)(2,1)S(1)}, u32[]{:S(2)}, u32[]{:S(2)}) collective-permute-start(bf16[528,768]{1,0:T(8,128)(2,1)S(1)} %get-tuple-element.104), channel_id=1, source_target_pairs={{0,4},{4,8},{8,12},{12,0},{1,5},{5,9},{9,13},{13,1},{2,6},{6,10},{... | collective-permute-start | bytes 2433032 | tf_op jit(solution)/shard_map/ppermute | solution.py:534
  324.4 16.1 %collective-permute-start.6 = (bf16[528,768]{1,0:T(8,128)(2,1)S(1)}, bf16[528,768]{1,0:T(8,128)(2,1)S(1)}, u32[]{:S(2)}, u32[]{:S(2)}) collective-permute-start(bf16[528,768]{1,0:T(8,128)(2,1)S(1)} %added.4), channel_id=1, source_target_pairs={{0,4},{4,8},{8,12},{12,0},{1,5},{5,9},{9,13},{13,1},{2,6},{6,10},{... | collective-permute-start | bytes 2433032 | tf_op jit(solution)/shard_map/ppermute | solution.py:534
  334.3 12.6 %collective-permute-start.9 = (bf16[528,768]{1,0:T(8,128)(2,1)S(1)}, bf16[528,768]{1,0:T(8,128)(2,1)S(1)}, u32[]{:S(2)}, u32[]{:S(2)}) collective-permute-start(bf16[528,768]{1,0:T(8,128)(2,1)S(1)} %added.5), channel_id=1, source_target_pairs={{0,12},{4,0},{8,4},{12,8},{1,13},{5,1},{9,5},{13,9},{2,14},{6,2},{... | collective-permute-start | bytes 2433032 | tf_op jit(solution)/shard_map/ppermute | solution.py:534
  (15 other events, 59.7 us)
Sparse Core Ops, SparseCore 0:
  41.3 68.1 all-gather.4
  111.2 68.8 all-gather.6

commit v3 on v2

--- a/solution.py
+++ b/solution.py
@@ -487,32 +487,34 @@
         for row, tail in zip(rows[1:], tails[1:]):
             mass = mass + masses_of(tail)
             total = total + row[...].astype(F32)
-        pick = lax.broadcasted_iota(jnp.int32, mass.shape, 0) == b
-        line = jnp.sum(jnp.where(pick, mass, 0.0), axis=0, keepdims=True)
-        share = jnp.broadcast_to(1.0 / line, (BLK, BLK)).T
-        out_ref[...] = (total * share[:, 0:1]).astype(BF16)
-
-    @pl.when(step < HALF)
+        for k in range(2):
+            pick = lax.broadcasted_iota(jnp.int32, mass.shape, 0) == 2 * b + k
+            line = jnp.sum(jnp.where(pick, mass, 0.0), axis=0, keepdims=True)
+            share = jnp.broadcast_to(1.0 / line, (BLK, BLK)).T
+            here = slice(k * BLK, (k + 1) * BLK)
+            out_ref[here, :] = (total[here, :] * share[:, 0:1]).astype(BF16)
+
+    @pl.when(step < HALF // 2)
     def _():
         give(ins[0:3], ins[6:9], step)
 
-    @pl.when(step >= HALF)
+    @pl.when(step >= HALF // 2)
     def _():
-        give(ins[3:6], ins[9:12], step - HALF)
+        give(ins[3:6], ins[9:12], step - HALF // 2)
 
 
 def mean_of(low, high):
     width = low[0].shape[1]
     loads, rows, tails = [*low, *high], [], []
-    for at in (lambda b: jnp.minimum(b, HALF - 1), lambda b: jnp.maximum(b - HALF, 0)):
-        rows += [pl.BlockSpec((BLK, width), lambda b, at=at: (at(b), 0))] * 3
+    for at in (lambda b: jnp.minimum(b, HALF // 2 - 1), lambda b: jnp.maximum(b - HALF // 2, 0)):
+        rows += [pl.BlockSpec((2 * BLK, width), lambda b, at=at: (at(b), 0))] * 3
         tails += [pl.BlockSpec((16, width), lambda b: (HALF * BLK // 16, 0))] * 3
     return pl.pallas_call(
         mean_kernel,
         out_shape=jax.ShapeDtypeStruct((OWN * BLK, width), BF16),
-        grid=(OWN,),
+        grid=(OWN // 2,),
         in_specs=rows + tails,
-        out_specs=pl.BlockSpec((BLK, width), lambda b: (b, 0)),
+        out_specs=pl.BlockSpec((2 * BLK, width), lambda b: (b, 0)),
         compiler_params=pltpu.CompilerParams(vmem_limit_bytes=16 << 20),
         name="mean_of",
     )(*loads, *loads)

time: 359 us -> 357 us (level)
  transfers between devices with their start and end apart: 22 -> 22, of which waited for: 11 -> 11; matrix products, arithmetic and copies ran while one was open for 1% -> 1% of each run, Pallas kernels for 14% -> 13%
where the time goes in v3:
time: 357 us; the launch traced here: 356 us
  blocking collectives  154 us (43%)
  Pallas kernels  67.1 us (19%)
  waiting for transfers between devices  57.5 us (16%)
  starting transfers between devices  43.1 us (12%)
  local copies, waits for them, and re-layouts  17.1 us (5%)
  between operations  14.6 us (4%)
    all_to_all x16, blocking collectives, exchanged(): return lax.all_to_all(copies, axis, split_axis=0, concat_axis=0, tiled=True)  154 us
    ppermute x12, waiting for transfers between devices, shifted(): lax.ppermute(value, axis, [(k, (k + away) % SIDE) for k in range(SIDE)])  32.4 us
    all_to_all x4, starting transfers between devices, exchanged(): return lax.all_to_all(copies, axis, split_axis=0, concat_axis=0, tiled=True)  19.5 us
    pallas_call x6, Pallas kernels, weighted_sums(): pl.pallas_call(functools.partial(sums_kernel, by_src), out_shape=(jax.Sha...  18 us
    all_to_all x4, waiting for transfers between devices, exchanged(): return lax.all_to_all(copies, axis, split_axis=0, concat_axis=0, tiled=True)  17.3 us
    ppermute x12, starting transfers between devices, shifted(): lax.ppermute(value, axis, [(k, (k + away) % SIDE) for k in range(SIDE)])  16.9 us
    pallas_call x6, Pallas kernels, fine_half(): pl.pallas_call(functools.partial(fine_half_kernel, first, last, given_at,...  14.5 us
    unnamed x50, local copies, waits for them, and re-layouts  13.9 us
  transfers between devices with their start and end apart: 22, of which 11 were waited for; matrix products, arithmetic and copies ran while one was open for 1% of the time, Pallas kernels for 13%

profile of v3, /device:TPU:0, one launch (start us, length us, event | category | flops | bytes accessed | tf_op | source)
XLA Modules:
  0.0 356.1 jit_solution(7791196657955318925)
XLA Ops:
  9.5 7.1 %all-to-all-start = ((bf16[16,64,768]{2,1,0:T(8,128)(2,1)}), bf16[16,64,768]{2,1,0:T(8,128)(2,1)S(1)}, u32[]{:S(2)}, u32[]{:S(2)}) async-start(bf16[16,64,768]{2,1,0:T(8,128)(2,1)} %broadcast_in_dim.3), calls=%async_computation | async-start | bytes 3145728 | tf_op jit(solution)/shard_map/all_to_all | solution.py:527
  27.5 5.4 %collective-permute-done.2.refs_2_ = bf16[2,96,512]{2,1,0:T(8,128)(2,1)S(1)} collective-permute-done((bf16[2,96,512]{2,1,0:T(8,128)(2,1)S(1)}, bf16[2,96,512]{2,1,0:T(8,128)(2,1)S(1)}, u32[]{:S(2)}, u32[]{:S(2)}) %collective-permute-start.2) | collective-permute-done | bytes 196640 | tf_op jit(solution)/shard_map/ppermute | solution.py:558
  32.9 8.3 %all-to-all-done = bf16[16,64,768]{2,1,0:T(8,128)(2,1)S(1)} async-done(((bf16[16,64,768]{2,1,0:T(8,128)(2,1)}), bf16[16,64,768]{2,1,0:T(8,128)(2,1)S(1)}, u32[]{:S(2)}, u32[]{:S(2)}) %all-to-all-start) | async-done | bytes 1572896 | tf_op jit(solution)/shard_map/all_to_all | solution.py:527
  53.8 9.0 %all-to-all-done.1.recv_ref = f32[16,33,128]{2,1,0:T(8,128)S(1)} async-done(((f32[16,33,128]{2,1,0:T(8,128)}), f32[16,33,128]{2,1,0:T(8,128)S(1)}, u32[]{:S(2)}, u32[]{:S(2)}) %all-to-all-start.1) | async-done | bytes 270368 | tf_op jit(solution)/shard_map/all_to_all | solution.py:527
  64.4 5.3 %all-to-all-start.2 = ((f32[8,4,128]{2,1,0:T(4,128)}), f32[8,4,128]{2,1,0:T(4,128)S(1)}, u32[]{:S(2)}, u32[]{:S(2)}) async-start(f32[8,4,128]{2,1,0:T(4,128)} %coarse_half.13), calls=%async_computation.2 | async-start | bytes 32768 | tf_op jit(solution)/shard_map/all_to_all | solution.py:527
  70.5 4.6 %entry_table.1.table_ref.refs_0_ = s32[768]{0:T(1024)} custom-call(s32[128]{0:T(128)} %convert_element_type.45.lists_ref, s32[4]{0:T(128)} %copy-done.13), custom_call_target="tpu_custom_call" | custom-call | tf_op jit(solution)/shard_map/entry_table/pallas_call | solution.py:212
  77.8 11.5 %all_to_all.100.recv_ref = f32[16,8,128]{2,1,0:T(8,128)S(1)} all-to-all(f32[16,8,128]{2,1,0:T(8,128)S(1)} %coarse_half.14), channel_id=1, replica_groups=mesh['wide'=8,'y'=4,'x'=4] {'y','x'}, dimensions={0} | all-to-all | bytes 131072 | tf_op jit(solution)/shard_map/all_to_all | solution.py:527
  90.2 10.0 %all_to_all.101.recv_ref = f32[8,4,128]{2,1,0:T(4,128)S(1)} all-to-all(f32[8,4,128]{2,1,0:T(4,128)S(1)} %coarse_half.15), channel_id=1, replica_groups=mesh['wide'=8,'y'=4,'x'=4] {'wide'}, dimensions={0} | all-to-all | bytes 32768 | tf_op jit(solution)/shard_map/all_to_all | solution.py:527
  101.2 10.9 %all_to_all.102.recv_ref = f32[16,8,128]{2,1,0:T(8,128)S(1)} all-to-all(f32[16,8,128]{2,1,0:T(8,128)S(1)} %coarse_half.16), channel_id=1, replica_groups=mesh['wide'=8,'y'=4,'x'=4] {'y','x'}, dimensions={0} | all-to-all | bytes 131072 | tf_op jit(solution)/shard_map/all_to_all | solution.py:527
  113.1 7.7 %all_to_all.103.recv_ref = f32[8,4,128]{2,1,0:T(4,128)S(1)} all-to-all(f32[8,4,128]{2,1,0:T(4,128)S(1)} %coarse_half.17), channel_id=1, replica_groups=mesh['wide'=8,'y'=4,'x'=4] {'wide'}, dimensions={0} | all-to-all | bytes 32768 | tf_op jit(solution)/shard_map/all_to_all | solution.py:527
  121.9 11.7 %all_to_all.104.recv_ref = f32[16,8,128]{2,1,0:T(8,128)S(1)} all-to-all(f32[16,8,128]{2,1,0:T(8,128)S(1)} %coarse_half.18), channel_id=1, replica_groups=mesh['wide'=8,'y'=4,'x'=4] {'y','x'}, dimensions={0} | all-to-all | bytes 131072 | tf_op jit(solution)/shard_map/all_to_all | solution.py:527
  134.6 7.7 %all_to_all.105.recv_ref = f32[8,4,128]{2,1,0:T(4,128)S(1)} all-to-all(f32[8,4,128]{2,1,0:T(4,128)S(1)} %coarse_half.19), channel_id=1, replica_groups=mesh['wide'=8,'y'=4,'x'=4] {'wide'}, dimensions={0} | all-to-all | bytes 32768 | tf_op jit(solution)/shard_map/all_to_all | solution.py:527
  143.3 11.4 %all_to_all.106.recv_ref = f32[16,8,128]{2,1,0:T(8,128)S(1)} all-to-all(f32[16,8,128]{2,1,0:T(8,128)S(1)} %coarse_half.20), channel_id=1, replica_groups=mesh['wide'=8,'y'=4,'x'=4] {'y','x'}, dimensions={0} | all-to-all | bytes 131072 | tf_op jit(solution)/shard_map/all_to_all | solution.py:527
  155.7 7.7 %all_to_all.107.recv_ref = f32[8,4,128]{2,1,0:T(4,128)S(1)} all-to-all(f32[8,4,128]{2,1,0:T(4,128)S(1)} %coarse_half.21), channel_id=1, replica_groups=mesh['wide'=8,'y'=4,'x'=4] {'wide'}, dimensions={0} | all-to-all | bytes 32768 | tf_op jit(solution)/shard_map/all_to_all | solution.py:527
  164.5 11.4 %all_to_all.108.recv_ref = f32[16,8,128]{2,1,0:T(8,128)S(1)} all-to-all(f32[16,8,128]{2,1,0:T(8,128)S(1)} %coarse_half.22), channel_id=1, replica_groups=mesh['wide'=8,'y'=4,'x'=4] {'y','x'}, dimensions={0} | all-to-all | bytes 131072 | tf_op jit(solution)/shard_map/all_to_all | solution.py:527
  176.9 8.2 %all_to_all.109.recv_ref = f32[8,4,128]{2,1,0:T(4,128)} all-to-all(f32[8,4,128]{2,1,0:T(4,128)S(1)} %coarse_half.23), channel_id=1, replica_groups=mesh['wide'=8,'y'=4,'x'=4] {'wide'}, dimensions={0} | all-to-all | bytes 32768 | tf_op jit(solution)/shard_map/all_to_all | solution.py:527
  195.6 4.9 %fine_costs.1 = (f32[52,128,128]{2,1,0:T(8,128)S(1)}, f32[52,128,128]{2,1,0:T(8,128)S(1)}) custom-call(s32[768]{0:T(1024)S(1)} %copy-done.10, bf16[32,128,768]{2,1,0:T(8,128)(2,1)S(1)} %bitcast.40, bf16[32,128,768]{2,1,0:T(8,128)(2,1)S(1)} %bitcast.34, f32[32,128]{1,0:T(8,128)S(1)} %get-tuple-element.81.xsq_ref, f32[32,128]{1,0:T(8,128)S(1)} %get-tuple-element.82.ysq_ref), custom_call_target="tpu_custom_call" | custom-call | tf_op jit(solution)/shard_map/fine_costs/pallas_call | solution.py:242
  204.2 4.1 %fine_half.6 = f32[4,32,128]{2,1,0:T(8,128)S(1)} custom-call(s32[768]{0:T(1024)S(1)} %copy-done.10, f32[64,128]{1,0:T(8,128)S(1)} %bitcast.51, s32[32,128]{1,0:T(8,128)S(1)} %get-tuple-element.78.refs_2_, f32[52,128,128]{2,1,0:T(8,128)S(1)} %copy-done.1), custom_call_target="tpu_custom_call" | custom-call | tf_op jit(solution)/shard_map/fine_half/pallas_call | solution.py:326
  208.3 10.3 %all_to_all.110.refs_1_ = f32[4,32,128]{2,1,0:T(8,128)S(1)} all-to-all(f32[4,32,128]{2,1,0:T(8,128)S(1)} %fine_half.6), channel_id=1, replica_groups=mesh['wide'=8,'y'=4,'x'=4] {'y'}, dimensions={0} | all-to-all | bytes 131072 | tf_op jit(solution)/shard_map/all_to_all | solution.py:527
  220.6 9.9 %all_to_all.111.refs_1_ = f32[4,32,128]{2,1,0:T(8,128)S(1)} all-to-all(f32[4,32,128]{2,1,0:T(8,128)S(1)} %fine_half.7), channel_id=1, replica_groups=mesh['wide'=8,'y'=4,'x'=4] {'x'}, dimensions={0} | all-to-all | bytes 131072 | tf_op jit(solution)/shard_map/all_to_all | solution.py:527
  232.7 8.0 %all_to_all.112.refs_1_ = f32[4,32,128]{2,1,0:T(8,128)S(1)} all-to-all(f32[4,32,128]{2,1,0:T(8,128)S(1)} %fine_half.8), channel_id=1, replica_groups=mesh['wide'=8,'y'=4,'x'=4] {'y'}, dimensions={0} | all-to-all | bytes 131072 | tf_op jit(solution)/shard_map/all_to_all | solution.py:527
  242.8 8.0 %all_to_all.113.refs_1_ = f32[4,32,128]{2,1,0:T(8,128)S(1)} all-to-all(f32[4,32,128]{2,1,0:T(8,128)S(1)} %fine_half.9), channel_id=1, replica_groups=mesh['wide'=8,'y'=4,'x'=4] {'x'}, dimensions={0} | all-to-all | bytes 131072 | tf_op jit(solution)/shard_map/all_to_all | solution.py:527
  252.9 8.3 %all_to_all.114.refs_1_ = f32[4,32,128]{2,1,0:T(8,128)S(1)} all-to-all(f32[4,32,128]{2,1,0:T(8,128)S(1)} %fine_half.10), channel_id=1, replica_groups=mesh['wide'=8,'y'=4,'x'=4] {'y'}, dimensions={0} | all-to-all | bytes 131072 | tf_op jit(solution)/shard_map/all_to_all | solution.py:527
  269.5 11.5 %all_to_all.115.trecv_ref = f32[4,32,128]{2,1,0:T(8,128)S(1)} all-to-all(f32[4,32,128]{2,1,0:T(8,128)S(1)} %get-tuple-element.86.mine_ref), channel_id=1, replica_groups=mesh['wide'=8,'y'=4,'x'=4] {'x'}, dimensions={0} | all-to-all | bytes 131072 | tf_op jit(solution)/shard_map/all_to_all | solution.py:527
  287.1 3.8 %weighted_sums.8 = (bf16[528,768]{1,0:T(8,128)(2,1)S(1)}, bf16[528,768]{1,0:T(8,128)(2,1)S(1)}, bf16[528,768]{1,0:T(8,128)(2,1)S(1)}, bf16[528,768]{1,0:T(8,128)(2,1)S(1)}) custom-call(s32[768]{0:T(1024)S(1)} %copy-done.10, s32[4]{0:T(128)S(1)} %copy-done.14, s32[4]{0:T(128)S(1)} %copy-done.17, f32[32,128]{1,0:T(8,128)S(1)} %get-tuple-element.85.s_ref.mine_ref.other_ref, ...), custom_call_target="tpu_custom_call" | custom-call | tf_op jit(solution)/shard_map/weighted_sums/pallas_call | solution.py:441
  294.3 3.8 %collective-permute-start.12 = (bf16[528,768]{1,0:T(8,128)(2,1)S(1)}, bf16[528,768]{1,0:T(8,128)(2,1)S(1)}, u32[]{:S(2)}, u32[]{:S(2)}) collective-permute-start(bf16[528,768]{1,0:T(8,128)(2,1)S(1)} %get-tuple-element.114), channel_id=1, source_target_pairs={{0,3},{1,0},{2,1},{3,2},{4,7},{5,4},{6,5},{7,6},{8,11},{9,8},{10,9... | collective-permute-start | bytes 2433032 | tf_op jit(solution)/shard_map/ppermute | solution.py:536
  298.1 4.1 %weighted_sums.10 = (bf16[528,768]{1,0:T(8,128)(2,1)S(1)}, bf16[528,768]{1,0:T(8,128)(2,1)S(1)}, bf16[528,768]{1,0:T(8,128)(2,1)S(1)}, bf16[528,768]{1,0:T(8,128)(2,1)S(1)}) custom-call(s32[768]{0:T(1024)S(1)} %copy-done.10, s32[4]{0:T(128)S(1)} %copy-done.14, s32[4]{0:T(128)S(1)} %copy-done.16, f32[32,128]{1,0:T(8,128)S(1)} %get-tuple-element.98.other_ref.mine_ref, ...), custom_call_target="tpu_custom_call" | custom-call | tf_op jit(solution)/shard_map/weighted_sums/pallas_call | solution.py:441
  305.8 5.2 %collective-permute-done.8.a_ref = bf16[528,768]{1,0:T(8,128)(2,1)S(1)} collective-permute-done((bf16[528,768]{1,0:T(8,128)(2,1)S(1)}, bf16[528,768]{1,0:T(8,128)(2,1)S(1)}, u32[]{:S(2)}, u32[]{:S(2)}) %collective-permute-start.8) | collective-permute-done | bytes 811040 | tf_op jit(solution)/shard_map/ppermute | solution.py:536
  311.0 4.0 %collective-permute-start.15 = (bf16[528,768]{1,0:T(8,128)(2,1)S(1)}, bf16[528,768]{1,0:T(8,128)(2,1)S(1)}, u32[]{:S(2)}, u32[]{:S(2)}) collective-permute-start(bf16[528,768]{1,0:T(8,128)(2,1)S(1)} %added.7), channel_id=1, source_target_pairs={{0,3},{1,0},{2,1},{3,2},{4,7},{5,4},{6,5},{7,6},{8,11},{9,8},{10,9... | collective-permute-start | bytes 2433032 | tf_op jit(solution)/shard_map/ppermute | solution.py:536
  316.2 8.2 %collective-permute-done.14.refs_4_.refs_10_ = bf16[528,768]{1,0:T(8,128)(2,1)S(1)} collective-permute-done((bf16[528,768]{1,0:T(8,128)(2,1)S(1)}, bf16[528,768]{1,0:T(8,128)(2,1)S(1)}, u32[]{:S(2)}, u32[]{:S(2)}) %collective-permute-start.14) | collective-permute-done | bytes 811040 | tf_op jit(solution)/shard_map/ppermute | solution.py:536
  324.5 9.8 %collective-permute-done.13.refs_2_.refs_8_ = bf16[528,768]{1,0:T(8,128)(2,1)S(1)} collective-permute-done((bf16[528,768]{1,0:T(8,128)(2,1)S(1)}, bf16[528,768]{1,0:T(8,128)(2,1)S(1)}, u32[]{:S(2)}, u32[]{:S(2)}) %collective-permute-start.13) | collective-permute-done | bytes 811040 | tf_op jit(solution)/shard_map/ppermute | solution.py:536
  340.4 6.5 %collective-permute-done.9.refs_5_.refs_11_ = bf16[528,768]{1,0:T(8,128)(2,1)S(1)} collective-permute-done((bf16[528,768]{1,0:T(8,128)(2,1)S(1)}, bf16[528,768]{1,0:T(8,128)(2,1)S(1)}, u32[]{:S(2)}, u32[]{:S(2)}) %collective-permute-start.9) | collective-permute-done | bytes 811040 | tf_op jit(solution)/shard_map/ppermute | solution.py:536
  (135 shorter events, 93.0 us)
Async XLA Ops:
  9.5 31.7 %all-to-all-start = ((bf16[16,64,768]{2,1,0:T(8,128)(2,1)}), bf16[16,64,768]{2,1,0:T(8,128)(2,1)S(1)}, u32[]{:S(2)}, u32[]{:S(2)}) async-start(bf16[16,64,768]{2,1,0:T(8,128)(2,1)} %broadcast_in_dim.3), calls=%async_computation | async-start | bytes 3145728 | tf_op jit(solution)/shard_map/all_to_all | solution.py:527
  16.7 9.8 %copy-start.22 = (s32[8,4]{0,1:T(4,128)S(1)}, s32[8,4]{0,1:T(4,128)}, u32[]{:S(2)}) copy-start(s32[8,4]{0,1:T(4,128)} %param.16) | copy-start | bytes 388
  16.7 173.3 %all-gather.5.cloned.1.call-start = ((), (), s32[]{:S(2)}) async-start(), calls=%async_computation.20 | async-start | bytes 7864320 | tf_op jit(solution)/shard_map/all_gather | solution.py:612
  16.7 1.4 collective-permute-start
  18.1 9.3 %collective-permute-start.1 = (bf16[2,96,512]{2,1,0:T(8,128)(2,1)S(1)}, bf16[2,96,512]{2,1,0:T(8,128)(2,1)S(1)}, u32[]{:S(2)}, u32[]{:S(2)}) collective-permute-start(bf16[2,96,512]{2,1,0:T(8,128)(2,1)S(1)} %pad_maximum_fusion.refs_0_), channel_id=1, source_target_pairs={{0,32},{16,48},{32,64},{48,80},{64,96},{80,112},{96,0},{112,16},{1... | collective-permute-start | bytes 589832 | tf_op jit(solution)/shard_map/ppermute | solution.py:558
  20.1 12.7 %collective-permute-start.2 = (bf16[2,96,512]{2,1,0:T(8,128)(2,1)S(1)}, bf16[2,96,512]{2,1,0:T(8,128)(2,1)S(1)}, u32[]{:S(2)}, u32[]{:S(2)}) collective-permute-start(bf16[2,96,512]{2,1,0:T(8,128)(2,1)S(1)} %pad_maximum_fusion.refs_0_), channel_id=1, source_target_pairs={{0,64},{16,80},{32,96},{48,112},{64,0},{80,16},{96,32},{112,48},{1... | collective-permute-start | bytes 589832 | tf_op jit(solution)/shard_map/ppermute | solution.py:558
  23.7 9.1 %collective-permute-start.3 = (bf16[2,96,512]{2,1,0:T(8,128)(2,1)S(1)}, bf16[2,96,512]{2,1,0:T(8,128)(2,1)S(1)}, u32[]{:S(2)}, u32[]{:S(2)}) collective-permute-start(bf16[2,96,512]{2,1,0:T(8,128)(2,1)S(1)} %pad_maximum_fusion.refs_0_), channel_id=1, source_target_pairs={{0,96},{16,112},{32,0},{48,16},{64,32},{80,48},{96,64},{112,80},{1... | collective-permute-start | bytes 589832 | tf_op jit(solution)/shard_map/ppermute | solution.py:558
  41.2 148.8 %all-gather.7.cloned.1.call-start = ((), (), s32[]{:S(2)}) async-start(), calls=%async_computation.21 | async-start | bytes 7864320 | tf_op jit(solution)/shard_map/all_gather | solution.py:611
  47.3 15.5 %copy-start.11 = (f32[1024]{0:T(1024)S(1)}, f32[1024]{0:T(1024)}, u32[]{:S(2)}) copy-start(f32[1024]{0:T(1024)} %param.20) | copy-start | bytes 12292
  50.2 12.6 %all-to-all-start.1 = ((f32[16,33,128]{2,1,0:T(8,128)}), f32[16,33,128]{2,1,0:T(8,128)S(1)}, u32[]{:S(2)}, u32[]{:S(2)}) async-start(f32[16,33,128]{2,1,0:T(8,128)} %coarse_half.12), calls=%async_computation.1 | async-start | bytes 655360 | tf_op jit(solution)/shard_map/all_to_all | solution.py:527
  64.4 10.7 %all-to-all-start.2 = ((f32[8,4,128]{2,1,0:T(4,128)}), f32[8,4,128]{2,1,0:T(4,128)S(1)}, u32[]{:S(2)}, u32[]{:S(2)}) async-start(f32[8,4,128]{2,1,0:T(4,128)} %coarse_half.13), calls=%async_computation.2 | async-start | bytes 32768 | tf_op jit(solution)/shard_map/all_to_all | solution.py:527
  163.4 26.6 %copy-start.10 = (s32[768]{0:T(1024)S(1)}, s32[768]{0:T(1024)}, u32[]{:S(2)}) copy-start(s32[768]{0:T(1024)} %entry_table.1.table_ref.refs_0_) | copy-start | bytes 9220
  186.5 15.7 %all-to-all-start.13 = ((f32[16,4,128]{2,1,0:T(4,128)}), f32[16,4,128]{2,1,0:T(4,128)S(1)}, u32[]{:S(2)}, u32[]{:S(2)}) async-start(f32[16,4,128]{2,1,0:T(4,128)} %coarse_end.1), calls=%async_computation.13 | async-start | bytes 65536 | tf_op jit(solution)/shard_map/all_to_all | solution.py:527
  230.6 51.6 %slice-start = ((s8[6291456]{0:T(1024)(128)(4,1)}), s8[4194304]{0:T(1024)(128)(4,1)S(1)}, s32[]{:S(2)}) async-start(s8[6291456]{0:T(1024)(128)(4,1)} %bitcast.35), calls=%async_computation.22 | async-start | bytes 8388608
  240.7 22.6 %copy-start.5 = (bf16[4096,768]{1,0:T(8,128)(2,1)S(1)}, bf16[4096,768]{1,0:T(8,128)(2,1)}, u32[]{:S(2)}) copy-start(bf16[4096,768]{1,0:T(8,128)(2,1)} %all-gather.5.cloned.1.call-done) | copy-start | bytes 18874372
  252.9 10.4 %copy-start.2 = (f32[52,128,128]{2,1,0:T(8,128)S(1)}, f32[52,128,128]{2,1,0:T(8,128)}, u32[]{:S(2)}) copy-start(f32[52,128,128]{2,1,0:T(8,128)} %copy-done) | copy-start | bytes 10223620
  252.9 10.4 %copy-start.14 = (s32[4]{0:T(128)S(1)}, s32[4]{0:T(128)}, u32[]{:S(2)}) copy-start(s32[4]{0:T(128)} %copy-done.13) | copy-start | bytes 52
  252.9 10.4 %copy-start.15 = (s32[2]{0:T(128)S(1)}, s32[2]{0:T(128)}, u32[]{:S(2)}) copy-start(s32[2]{0:T(128)} %constant.60.clone.picks_ref) | copy-start | bytes 28
  261.2 20.9 %slice-start.1 = ((s8[6291456]{0:T(1024)(128)(4,1)}), s8[2097152]{0:T(1024)(128)(4,1)S(1)}, s32[]{:S(2)}) async-start(s8[6291456]{0:T(1024)(128)(4,1)} %bitcast.35), calls=%async_computation.23 | async-start | bytes 4194304
  266.2 36.0 %collective-permute-start.10 = (bf16[528,768]{1,0:T(8,128)(2,1)S(1)}, bf16[528,768]{1,0:T(8,128)(2,1)S(1)}, u32[]{:S(2)}, u32[]{:S(2)}) collective-permute-start(bf16[528,768]{1,0:T(8,128)(2,1)S(1)} %get-tuple-element.111), channel_id=1, source_target_pairs={{0,1},{1,2},{2,3},{3,0},{4,5},{5,6},{6,7},{7,4},{8,9},{9,10},{10,1... | collective-permute-start | bytes 2433032 | tf_op jit(solution)/shard_map/ppermute | solution.py:536
  266.3 36.0 %collective-permute-start.11 = (bf16[528,768]{1,0:T(8,128)(2,1)S(1)}, bf16[528,768]{1,0:T(8,128)(2,1)S(1)}, u32[]{:S(2)}, u32[]{:S(2)}) collective-permute-start(bf16[528,768]{1,0:T(8,128)(2,1)S(1)} %get-tuple-element.112), channel_id=1, source_target_pairs={{0,3},{1,0},{2,1},{3,2},{4,7},{5,4},{6,5},{7,6},{8,11},{9,8},{10,9... | collective-permute-start | bytes 2433032 | tf_op jit(solution)/shard_map/ppermute | solution.py:536
  287.1 10.9 %copy-start.16 = (s32[4]{0:T(128)S(1)}, s32[4]{0:T(128)}, u32[]{:S(2)}) copy-start(s32[4]{0:T(128)} %constant.63.clone.picks_ref) | copy-start | bytes 52
  291.0 13.5 %collective-permute-start.5 = (bf16[528,768]{1,0:T(8,128)(2,1)S(1)}, bf16[528,768]{1,0:T(8,128)(2,1)S(1)}, u32[]{:S(2)}, u32[]{:S(2)}) collective-permute-start(bf16[528,768]{1,0:T(8,128)(2,1)S(1)} %get-tuple-element.101), channel_id=1, source_target_pairs={{0,4},{4,8},{8,12},{12,0},{1,5},{5,9},{9,13},{13,1},{2,6},{6,10},{... | collective-permute-start | bytes 2433032 | tf_op jit(solution)/shard_map/ppermute | solution.py:536
  292.7 18.2 %collective-permute-start.8 = (bf16[528,768]{1,0:T(8,128)(2,1)S(1)}, bf16[528,768]{1,0:T(8,128)(2,1)S(1)}, u32[]{:S(2)}, u32[]{:S(2)}) collective-permute-start(bf16[528,768]{1,0:T(8,128)(2,1)S(1)} %get-tuple-element.105), channel_id=1, source_target_pairs={{0,12},{4,0},{8,4},{12,8},{1,13},{5,1},{9,5},{13,9},{2,14},{6,2},{... | collective-permute-start | bytes 2433032 | tf_op jit(solution)/shard_map/ppermute | solution.py:536
  294.3 20.9 %collective-permute-start.12 = (bf16[528,768]{1,0:T(8,128)(2,1)S(1)}, bf16[528,768]{1,0:T(8,128)(2,1)S(1)}, u32[]{:S(2)}, u32[]{:S(2)}) collective-permute-start(bf16[528,768]{1,0:T(8,128)(2,1)S(1)} %get-tuple-element.114), channel_id=1, source_target_pairs={{0,3},{1,0},{2,1},{3,2},{4,7},{5,4},{6,5},{7,6},{8,11},{9,8},{10,9... | collective-permute-start | bytes 2433032 | tf_op jit(solution)/shard_map/ppermute | solution.py:536
  302.2 22.2 %collective-permute-start.14 = (bf16[528,768]{1,0:T(8,128)(2,1)S(1)}, bf16[528,768]{1,0:T(8,128)(2,1)S(1)}, u32[]{:S(2)}, u32[]{:S(2)}) collective-permute-start(bf16[528,768]{1,0:T(8,128)(2,1)S(1)} %get-tuple-element.119), channel_id=1, source_target_pairs={{0,1},{1,2},{2,3},{3,0},{4,5},{5,6},{6,7},{7,4},{8,9},{9,10},{10,1... | collective-permute-start | bytes 2433032 | tf_op jit(solution)/shard_map/ppermute | solution.py:536
  302.7 31.6 %collective-permute-start.13 = (bf16[528,768]{1,0:T(8,128)(2,1)S(1)}, bf16[528,768]{1,0:T(8,128)(2,1)S(1)}, u32[]{:S(2)}, u32[]{:S(2)}) collective-permute-start(bf16[528,768]{1,0:T(8,128)(2,1)S(1)} %added.6), channel_id=1, source_target_pairs={{0,1},{1,2},{2,3},{3,0},{4,5},{5,6},{6,7},{7,4},{8,9},{9,10},{10,1... | collective-permute-start | bytes 2433032 | tf_op jit(solution)/shard_map/ppermute | solution.py:536
  304.5 34.4 %collective-permute-start.4 = (bf16[528,768]{1,0:T(8,128)(2,1)S(1)}, bf16[528,768]{1,0:T(8,128)(2,1)S(1)}, u32[]{:S(2)}, u32[]{:S(2)}) collective-permute-start(bf16[528,768]{1,0:T(8,128)(2,1)S(1)} %get-tuple-element.100), channel_id=1, source_target_pairs={{0,12},{4,0},{8,4},{12,8},{1,13},{5,1},{9,5},{13,9},{2,14},{6,2},{... | collective-permute-start | bytes 2433032 | tf_op jit(solution)/shard_map/ppermute | solution.py:536
  311.0 25.6 %collective-permute-start.15 = (bf16[528,768]{1,0:T(8,128)(2,1)S(1)}, bf16[528,768]{1,0:T(8,128)(2,1)S(1)}, u32[]{:S(2)}, u32[]{:S(2)}) collective-permute-start(bf16[528,768]{1,0:T(8,128)(2,1)S(1)} %added.7), channel_id=1, source_target_pairs={{0,3},{1,0},{2,1},{3,2},{4,7},{5,4},{6,5},{7,6},{8,11},{9,8},{10,9... | collective-permute-start | bytes 2433032 | tf_op jit(solution)/shard_map/ppermute | solution.py:536
  315.2 23.7 %collective-permute-start.7 = (bf16[528,768]{1,0:T(8,128)(2,1)S(1)}, bf16[528,768]{1,0:T(8,128)(2,1)S(1)}, u32[]{:S(2)}, u32[]{:S(2)}) collective-permute-start(bf16[528,768]{1,0:T(8,128)(2,1)S(1)} %get-tuple-element.104), channel_id=1, source_target_pairs={{0,4},{4,8},{8,12},{12,0},{1,5},{5,9},{9,13},{13,1},{2,6},{6,10},{... | collective-permute-start | bytes 2433032 | tf_op jit(solution)/shard_map/ppermute | solution.py:536
  324.4 16.1 %collective-permute-start.6 = (bf16[528,768]{1,0:T(8,128)(2,1)S(1)}, bf16[528,768]{1,0:T(8,128)(2,1)S(1)}, u32[]{:S(2)}, u32[]{:S(2)}) collective-permute-start(bf16[528,768]{1,0:T(8,128)(2,1)S(1)} %added.4), channel_id=1, source_target_pairs={{0,4},{4,8},{8,12},{12,0},{1,5},{5,9},{9,13},{13,1},{2,6},{6,10},{... | collective-permute-start | bytes 2433032 | tf_op jit(solution)/shard_map/ppermute | solution.py:536
  334.3 12.6 %collective-permute-start.9 = (bf16[528,768]{1,0:T(8,128)(2,1)S(1)}, bf16[528,768]{1,0:T(8,128)(2,1)S(1)}, u32[]{:S(2)}, u32[]{:S(2)}) collective-permute-start(bf16[528,768]{1,0:T(8,128)(2,1)S(1)} %added.5), channel_id=1, source_target_pairs={{0,12},{4,0},{8,4},{12,8},{1,13},{5,1},{9,5},{13,9},{2,14},{6,2},{... | collective-permute-start | bytes 2433032 | tf_op jit(solution)/shard_map/ppermute | solution.py:536
  (15 other events, 59.7 us)
Sparse Core Ops, SparseCore 0:
  41.3 68.1 all-gather.4
  111.2 68.8 all-gather.6
